TPU v7x, 32 devices: a whole 2x2x4 slice. The times are simulated.
32 devices in a mesh: items: 16 (over z, x, core), heads: 2 (over y).
Axes of the slice: x: 2, y: 2, z: 4, core: 2. Of those that a mesh axis runs over, the one named last changes fastest.
Arguments:
- tokens: bfloat16 [32, 512, 768], P(('items', 'heads')), may hold values from -6 to 6
- earlier: bfloat16 [32, 512, 768], P(('items', 'heads')), may hold values from -6 to 6
- coeffs: float32 [32, 256, 768], P(('items', 'heads')), may hold values from -6 to 6
- present: int32 [32], P(('items', 'heads')), may hold values 0 or 1
- sample_at: int32 [32, 512], P(('items', 'heads')), may hold values from 0 to 1023
- w_qkv: float32 [3, 768, 768], P(None, 'items', 'heads'), may hold values from -0.21875 to 0.21875
- w_out: float32 [768, 768], P('heads', 'items'), may hold values from -1.25 to 1.25
- w_up: float32 [768, 3072], P('items', 'heads'), may hold values from -0.21875 to 0.21875
- w_down: float32 [3072, 768], P('heads', 'items'), may hold values from -0.109375 to 0.109375
- gain_attn: float32 [768], P('items'), may hold values from 0.25 to 1.75
- gain_mlp: float32 [768], P('items'), may hold values from 0.25 to 1.75
- w_mean: float32 [12, 256], P('heads', 'items'), may hold values from -0.375 to 0.375
- w_var: float32 [12, 256], P('heads', 'items'), may hold values from -0.375 to 0.375
- cotangent: bfloat16 [32, 512, 768], P(('items', 'heads')), may hold values from -6 to 6
Outputs:
- output: bfloat16 [32, 512, 768], P(('items', 'heads'))
- grad_tokens: float32 [32, 512, 768], P(('items', 'heads'))
- grad_coeffs: float32 [32, 256, 768], P(('items', 'heads'))
- grad_w_qkv: float32 [3, 768, 768], P(None, 'items', 'heads')
- grad_w_out: float32 [768, 768], P('heads', 'items')
- grad_w_up: float32 [768, 3072], P('items', 'heads')
- grad_w_down: float32 [3072, 768], P('heads', 'items')
- grad_gain_attn: float32 [768], P(('items', 'heads'))
- grad_gain_mlp: float32 [768], P(('items', 'heads'))
- grad_w_mean: float32 [12, 256], P('heads', 'items')
- grad_w_var: float32 [12, 256], P('heads', 'items')
Inputs may be any that keep to these rules, and one draw needn't show every extreme that they name: `sample_at`: grid points, out of 1024, at which an item's old memory is sampled. `present`: 1 where the item carries old memory.
All inputs are finite; a program needn't handle non-finite values. No bound on the sum of `present` on one device may be relied on, other than what follows from the above.
Results may differ from a plain program's by a relative error of at most 0.017.
The roundings to bfloat16 on the way count: a program that leaves them out, or rounds other values in their place, can miss the bound.
Values may be sent and summed in bfloat16 or wider, within the bound.
No kernel may reach another device: no remote copies, remote signals or barrier semaphores. Data moves between devices by JAX's collectives and lax.ppermute only.
A program may use at most 128 MiB of HBM per device.

v0:
```python
import math

import jax
import jax.numpy as jnp
from jax import lax
from jax.sharding import PartitionSpec as P

HD = 64
GRID = 1024


EPSILON = 1e-05
VAR_SCALE = 0.01
RIDGE = 1.0
HIGHEST = lax.Precision.HIGHEST


def layer_norm(values, gain_vec):
    row_mean = jnp.mean(values, axis=-1, keepdims=True)
    centred = values - row_mean
    spread = jnp.mean(centred * centred, axis=-1, keepdims=True)
    return centred * lax.rsqrt(spread + EPSILON) * gain_vec


def basis_at(points, basis_count):
    centers = (jnp.arange(basis_count, dtype=jnp.float32) + 0.5) / basis_count
    offset = points[..., None] - centers
    return jnp.exp(-offset * offset * (0.5 * basis_count * basis_count))


def ridge_table(basis_count, samples):
    points = (jnp.arange(samples, dtype=jnp.float32) + 0.5) / samples
    design = basis_at(points, basis_count)
    gram_matrix = jnp.dot(design.T, design, precision=HIGHEST) + RIDGE * jnp.eye(
        basis_count, dtype=jnp.float32
    )
    factor = jnp.linalg.cholesky(gram_matrix)
    return jax.scipy.linalg.cho_solve((factor, True), design.T)


def density(raw_scores, w_mean, w_var):
    basis_count = w_mean.shape[-1]
    scaled = raw_scores * 0.125
    centers = (jnp.arange(basis_count, dtype=jnp.float32) + 0.5) / basis_count
    middle = jax.nn.sigmoid(jnp.dot(scaled, w_mean, precision=HIGHEST))
    variance = VAR_SCALE * jax.nn.softplus(jnp.dot(scaled, w_var, precision=HIGHEST)) + 1.0 / (
        basis_count * basis_count
    )
    offset = middle[:, None] - centers
    return (
        jnp.exp(-offset * offset / (2.0 * variance[:, None]))
        * lax.rsqrt(2.0 * math.pi * variance)[:, None]
        / basis_count
    )


def gelu_tanh(values):
    return jax.nn.gelu(values, approximate=True)


def split_heads(values, local_heads):
    groups, length, _ = values.shape
    return (
        values.reshape(groups, length, local_heads, -1)
        .transpose(0, 2, 1, 3)
        .reshape(groups * local_heads, length, -1)
    )


def join_heads(values, local_heads):
    flat_count, length, head_width = values.shape
    return (
        values.reshape(flat_count // local_heads, local_heads, length, head_width)
        .transpose(0, 2, 1, 3)
        .reshape(flat_count // local_heads, length, local_heads * head_width)
    )


def head_scores(queries, keys_all):
    length = queries.shape[0]
    allowed = jnp.arange(2 * length)[None, :] <= length + jnp.arange(length)[:, None]
    raw_scores = jnp.einsum("sd,td->st", queries, keys_all, preferred_element_type=jnp.float32)
    return jnp.where(allowed, raw_scores * 0.125, -1e30)


def head_forward(inputs_row):
    queries, keys_all, values_all, mem_keys, mem_values, w_mean, w_var = inputs_row
    scores = head_scores(queries, keys_all)
    row_max = jnp.max(scores, axis=-1, keepdims=True)
    row_sum = jnp.sum(jnp.exp(scores - row_max), axis=-1, keepdims=True)
    log_sum = row_max + jnp.log(row_sum)
    attn_probs = jnp.exp(scores - log_sum).astype(jnp.bfloat16)
    near_part = jnp.dot(attn_probs, values_all, preferred_element_type=jnp.float32)
    mem_raw = jnp.einsum("sd,jd->sj", queries, mem_keys, preferred_element_type=jnp.float32)
    weights_mem = density(mem_raw, w_mean, w_var).astype(jnp.bfloat16)
    recall = jnp.dot(weights_mem, mem_values, preferred_element_type=jnp.float32)
    return (near_part + recall, log_sum[:, 0])


def head_backward(inputs_row):
    queries, keys_all, values_all, mem_keys, mem_values, w_mean, w_var, log_sum, grad_ctx = (
        inputs_row
    )
    scores = head_scores(queries, keys_all)
    attn_probs = jnp.exp(scores - log_sum[:, None])
    grad_probs = jnp.einsum("sd,td->st", grad_ctx, values_all, preferred_element_type=jnp.float32)
    row_inner = jnp.sum(attn_probs * grad_probs, axis=-1, keepdims=True)
    grad_raw = (0.125 * attn_probs * (grad_probs - row_inner)).astype(jnp.bfloat16)
    grad_queries = jnp.dot(grad_raw, keys_all, preferred_element_type=jnp.float32)
    grad_keys = jnp.einsum("st,sd->td", grad_raw, queries, preferred_element_type=jnp.float32)
    grad_values = jnp.einsum(
        "st,sd->td", attn_probs.astype(jnp.bfloat16), grad_ctx, preferred_element_type=jnp.float32
    )
    mem_raw = jnp.einsum("sd,jd->sj", queries, mem_keys, preferred_element_type=jnp.float32)
    weights_mem, pull_back = jax.vjp(density, mem_raw, w_mean, w_var)
    grad_weights = jnp.einsum("sd,jd->sj", grad_ctx, mem_values, preferred_element_type=jnp.float32)
    grad_mem_raw, grad_mean, grad_var = pull_back(grad_weights)
    grad_mem_raw = grad_mem_raw.astype(jnp.bfloat16)
    grad_queries = grad_queries + jnp.dot(
        grad_mem_raw, mem_keys, preferred_element_type=jnp.float32
    )
    grad_mem_keys = jnp.einsum(
        "sj,sd->jd", grad_mem_raw, queries, preferred_element_type=jnp.float32
    )
    grad_mem_values = jnp.einsum(
        "sj,sd->jd", weights_mem.astype(jnp.bfloat16), grad_ctx, preferred_element_type=jnp.float32
    )
    return (
        grad_queries,
        grad_keys,
        grad_values,
        grad_mem_keys,
        grad_mem_values,
        grad_mean,
        grad_var,
    )


def gather_weights(params):
    w_qkv, w_out, w_up, w_down, gain_attn, gain_mlp, w_mean, w_var = params
    return (
        lax.all_gather(w_qkv.astype(jnp.bfloat16), "items", axis=1, tiled=True),
        lax.all_gather(w_out.astype(jnp.bfloat16), "items", axis=1, tiled=True),
        lax.all_gather(w_up.astype(jnp.bfloat16), "items", axis=0, tiled=True),
        lax.all_gather(w_down.astype(jnp.bfloat16), "items", axis=1, tiled=True),
        lax.all_gather(gain_attn.astype(jnp.bfloat16), "items", axis=0, tiled=True),
        lax.all_gather(gain_mlp.astype(jnp.bfloat16), "items", axis=0, tiled=True),
        lax.all_gather(w_mean.astype(jnp.bfloat16), "items", axis=1, tiled=True),
        lax.all_gather(w_var.astype(jnp.bfloat16), "items", axis=1, tiled=True),
    )


def forward(tokens, earlier, coeffs, present, sample_at, params):
    qkv_low, out_low, up_low, down_low, gain_one, gain_two, mean_low, var_low = gather_weights(
        params
    )
    gain_attn = gain_one.astype(jnp.float32)
    gain_mlp = gain_two.astype(jnp.float32)
    w_mean = mean_low.astype(jnp.float32)
    w_var = var_low.astype(jnp.float32)
    local_heads = qkv_low.shape[2] // HD
    length = tokens.shape[1]
    basis_count = coeffs.shape[1]
    ridge = ridge_table(basis_count, 2 * length).astype(jnp.bfloat16)
    normed_own = layer_norm(tokens.astype(jnp.float32), gain_attn).astype(jnp.bfloat16)
    past_own = layer_norm(earlier.astype(jnp.float32), gain_attn).astype(jnp.bfloat16)
    old_basis = basis_at((sample_at.astype(jnp.float32) + 0.5) / GRID, basis_count).astype(
        jnp.bfloat16
    )
    carried = jnp.einsum(
        "isj,ijd->isd", old_basis, coeffs.astype(jnp.bfloat16), preferred_element_type=jnp.float32
    )
    samples = (present.astype(jnp.float32)[:, None, None] * carried).astype(jnp.bfloat16)
    memory_own = jnp.einsum(
        "jp,ipd->ijd",
        ridge,
        jnp.concatenate([samples, past_own], axis=1),
        preferred_element_type=jnp.float32,
    ).astype(jnp.bfloat16)
    normed, normed_past, memory = (
        lax.all_gather(normed_own, "heads", axis=0, tiled=True),
        lax.all_gather(past_own, "heads", axis=0, tiled=True),
        lax.all_gather(memory_own, "heads", axis=0, tiled=True),
    )
    current = jnp.einsum(
        "isd,cde->cise", normed, qkv_low, preferred_element_type=jnp.float32
    ).astype(jnp.bfloat16)
    past_kv = jnp.einsum(
        "isd,cde->cise", normed_past, qkv_low[1:], preferred_element_type=jnp.float32
    ).astype(jnp.bfloat16)
    mem_kv = jnp.einsum(
        "ijd,cde->cije", memory, qkv_low[1:], preferred_element_type=jnp.float32
    ).astype(jnp.bfloat16)
    groups = normed.shape[0]
    head_inputs = (
        split_heads(current[0], local_heads),
        split_heads(jnp.concatenate([past_kv[0], current[1]], axis=1), local_heads),
        split_heads(jnp.concatenate([past_kv[1], current[2]], axis=1), local_heads),
        split_heads(mem_kv[0], local_heads),
        split_heads(mem_kv[1], local_heads),
        jnp.tile(w_mean, (groups, 1)),
        jnp.tile(w_var, (groups, 1)),
    )
    mixed, log_sums = lax.map(head_forward, head_inputs)
    context = join_heads(mixed, local_heads).astype(jnp.bfloat16)
    attn_part = jnp.einsum("ise,ed->isd", context, out_low, preferred_element_type=jnp.float32)
    hidden = tokens.astype(jnp.float32) + lax.psum_scatter(
        attn_part.astype(jnp.bfloat16), "heads", scatter_dimension=0, tiled=True
    ).astype(jnp.float32)
    normed_mlp_own = layer_norm(hidden, gain_mlp).astype(jnp.bfloat16)
    normed_mlp = lax.all_gather(normed_mlp_own, "heads", axis=0, tiled=True)
    pre_act = jnp.einsum("isd,df->isf", normed_mlp, up_low, preferred_element_type=jnp.float32)
    activation = gelu_tanh(pre_act).astype(jnp.bfloat16)
    mlp_part = jnp.einsum("isf,fd->isd", activation, down_low, preferred_element_type=jnp.float32)
    output = (
        hidden
        + lax.psum_scatter(
            mlp_part.astype(jnp.bfloat16), "heads", scatter_dimension=0, tiled=True
        ).astype(jnp.float32)
    ).astype(jnp.bfloat16)
    saved = (
        qkv_low,
        out_low,
        up_low,
        down_low,
        gain_attn,
        gain_mlp,
        ridge,
        old_basis,
        normed,
        normed_past,
        memory,
        head_inputs,
        log_sums,
        context,
        hidden,
        normed_mlp,
        pre_act,
        activation,
    )
    return (output, saved)


def backward(saved, tokens, earlier, present, cotangent):
    (
        qkv_low,
        out_low,
        up_low,
        down_low,
        gain_attn,
        gain_mlp,
        ridge,
        old_basis,
        normed,
        normed_past,
        memory,
        head_inputs,
        log_sums,
        context,
        hidden,
        normed_mlp,
        pre_act,
        activation,
    ) = saved
    local_heads = qkv_low.shape[2] // HD
    length = tokens.shape[1]
    groups = normed.shape[0]
    grad_out = lax.all_gather(cotangent, "heads", axis=0, tiled=True)
    grad_w_down = jnp.einsum(
        "isf,isd->fd", activation, grad_out, preferred_element_type=jnp.float32
    )
    grad_act = jnp.einsum("isd,fd->isf", grad_out, down_low, preferred_element_type=jnp.float32)
    _, gelu_pull = jax.vjp(gelu_tanh, pre_act)
    grad_pre = gelu_pull(grad_act)[0].astype(jnp.bfloat16)
    grad_w_up = jnp.einsum("isd,isf->df", normed_mlp, grad_pre, preferred_element_type=jnp.float32)
    mlp_term = jnp.einsum("isf,df->isd", grad_pre, up_low, preferred_element_type=jnp.float32)
    grad_normed_mlp = lax.psum_scatter(
        mlp_term.astype(jnp.bfloat16), "heads", scatter_dimension=0, tiled=True
    ).astype(jnp.float32)
    _, second_pull = jax.vjp(layer_norm, hidden, gain_mlp)
    grad_hidden_norm, grad_gain_mlp = second_pull(grad_normed_mlp)
    grad_hidden = cotangent.astype(jnp.float32) + grad_hidden_norm
    grad_branch = lax.all_gather(grad_hidden.astype(jnp.bfloat16), "heads", axis=0, tiled=True)
    grad_w_out = jnp.einsum("ise,isd->ed", context, grad_branch, preferred_element_type=jnp.float32)
    grad_context = jnp.einsum(
        "isd,ed->ise", grad_branch, out_low, preferred_element_type=jnp.float32
    ).astype(jnp.bfloat16)
    back_inputs = head_inputs + (log_sums, split_heads(grad_context, local_heads))
    grad_queries, grad_keys, grad_values, grad_mem_keys, grad_mem_values, grad_mean, grad_var = (
        lax.map(head_backward, back_inputs)
    )
    grad_keys = join_heads(grad_keys, local_heads)
    grad_values = join_heads(grad_values, local_heads)
    grad_now = jnp.stack(
        [join_heads(grad_queries, local_heads), grad_keys[:, length:], grad_values[:, length:]]
    ).astype(jnp.bfloat16)
    grad_past = jnp.stack([grad_keys[:, :length], grad_values[:, :length]]).astype(jnp.bfloat16)
    grad_mem = jnp.stack(
        [join_heads(grad_mem_keys, local_heads), join_heads(grad_mem_values, local_heads)]
    ).astype(jnp.bfloat16)
    grad_w_qkv = jnp.einsum("isd,cise->cde", normed, grad_now, preferred_element_type=jnp.float32)
    extra_terms = jnp.einsum(
        "isd,cise->cde", normed_past, grad_past, preferred_element_type=jnp.float32
    )
    extra_terms = extra_terms + jnp.einsum(
        "ijd,cije->cde", memory, grad_mem, preferred_element_type=jnp.float32
    )
    grad_w_qkv = jnp.concatenate([grad_w_qkv[:1], grad_w_qkv[1:] + extra_terms], axis=0)
    grad_mean = jnp.sum(grad_mean.reshape(groups, local_heads, -1), axis=0)
    grad_var = jnp.sum(grad_var.reshape(groups, local_heads, -1), axis=0)
    normed_term = jnp.einsum("cise,cde->isd", grad_now, qkv_low, preferred_element_type=jnp.float32)
    past_term = jnp.einsum(
        "cise,cde->isd", grad_past, qkv_low[1:], preferred_element_type=jnp.float32
    )
    memory_term = jnp.einsum(
        "cije,cde->ijd", grad_mem, qkv_low[1:], preferred_element_type=jnp.float32
    )
    grad_normed, grad_normed_past, grad_memory = (
        lax.psum_scatter(
            normed_term.astype(jnp.bfloat16), "heads", scatter_dimension=0, tiled=True
        ).astype(jnp.float32),
        lax.psum_scatter(
            past_term.astype(jnp.bfloat16), "heads", scatter_dimension=0, tiled=True
        ).astype(jnp.float32),
        lax.psum_scatter(
            memory_term.astype(jnp.bfloat16), "heads", scatter_dimension=0, tiled=True
        ).astype(jnp.float32),
    )
    grad_fit = jnp.einsum(
        "jp,ijd->ipd", ridge, grad_memory.astype(jnp.bfloat16), preferred_element_type=jnp.float32
    )
    grad_samples = grad_fit[:, :length].astype(jnp.bfloat16)
    grad_coeffs = present.astype(jnp.float32)[:, None, None] * jnp.einsum(
        "isj,isd->ijd", old_basis, grad_samples, preferred_element_type=jnp.float32
    )
    _, first_pull = jax.vjp(layer_norm, tokens.astype(jnp.float32), gain_attn)
    grad_tokens_norm, gain_from_tokens = first_pull(grad_normed)
    _, past_pull = jax.vjp(layer_norm, earlier.astype(jnp.float32), gain_attn)
    _, gain_from_past = past_pull(grad_normed_past + grad_fit[:, length:])
    grad_tokens = grad_hidden + grad_tokens_norm
    weight_grads = (
        lax.psum_scatter(grad_w_qkv, "items", scatter_dimension=1, tiled=True),
        lax.psum_scatter(grad_w_out, "items", scatter_dimension=1, tiled=True),
        lax.psum_scatter(grad_w_up, "items", scatter_dimension=0, tiled=True),
        lax.psum_scatter(grad_w_down, "items", scatter_dimension=1, tiled=True),
        lax.psum_scatter(grad_mean, "items", scatter_dimension=1, tiled=True),
        lax.psum_scatter(grad_var, "items", scatter_dimension=1, tiled=True),
    )
    gain_grads = (
        lax.psum_scatter(
            gain_from_tokens + gain_from_past, ("items", "heads"), scatter_dimension=0, tiled=True
        ),
        lax.psum_scatter(grad_gain_mlp, ("items", "heads"), scatter_dimension=0, tiled=True),
    )
    return (
        grad_tokens,
        grad_coeffs,
        weight_grads[0],
        weight_grads[1],
        weight_grads[2],
        weight_grads[3],
        gain_grads[0],
        gain_grads[1],
        weight_grads[4],
        weight_grads[5],
    )


def shards(
    tokens,
    earlier,
    coeffs,
    present,
    sample_at,
    w_qkv,
    w_out,
    w_up,
    w_down,
    gain_attn,
    gain_mlp,
    w_mean,
    w_var,
    cotangent,
):
    params = (w_qkv, w_out, w_up, w_down, gain_attn, gain_mlp, w_mean, w_var)
    output, saved = forward(tokens, earlier, coeffs, present, sample_at, params)
    fresh_inputs = lax.optimization_barrier((tokens, earlier, coeffs, params, cotangent))
    _, saved = forward(
        fresh_inputs[0], fresh_inputs[1], fresh_inputs[2], present, sample_at, fresh_inputs[3]
    )
    gradients = backward(saved, tokens, earlier, present, cotangent)
    return (output,) + gradients


def solution(mesh):
    in_specs = (
        P(("items", "heads"), None, None),
        P(("items", "heads"), None, None),
        P(("items", "heads"), None, None),
        P(("items", "heads")),
        P(("items", "heads"), None),
        P(None, "items", "heads"),
        P("heads", "items"),
        P("items", "heads"),
        P("heads", "items"),
        P("items"),
        P("items"),
        P("heads", "items"),
        P("heads", "items"),
        P(("items", "heads"), None, None),
    )
    out_specs = (
        P(("items", "heads"), None, None),
        P(("items", "heads"), None, None),
        P(("items", "heads"), None, None),
        P(None, "items", "heads"),
        P("heads", "items"),
        P("items", "heads"),
        P("heads", "items"),
        P(("items", "heads")),
        P(("items", "heads")),
        P("heads", "items"),
        P("heads", "items"),
    )
    return jax.shard_map(shards, mesh=mesh, in_specs=in_specs, out_specs=out_specs, check_vma=False)
```

profile of v0, /device:TPU:0, one launch (start us, length us, event | category | flops | bytes accessed | tf_op | source)
XLA Modules:
  0.0 1793.8 jit_solution(6639928590878580853)
XLA Ops:
  14.6 36.4 %all-reduce.9 = (bf16[768]{0:T(1024)(128)(2,1)}, bf16[768]{0:T(1024)(128)(2,1)S(1)}, bf16[768]{0:T(1024)(128)(2,1)}, bf16[768]{0:T(1024)(128)(2,1)}) all-reduce(bf16[768]{0:T(1024)(128)(2,1)S(1)} %dynamic-update-slice.8, bf16[768]{0:T(1024)(128)(2,1)S(1)} %dynamic-update-slice.10, ...), channel_id=1, replica_groups=mesh['items'=16,'heads'=2] {'items'}, use_global_device_ids=true, to_apply=%add.1 | all-reduce | flops 3072 | bytes 12288
  100.4 20.5 %custom-call.14 = f32[2,128,128]{1,2,0:T(8,128)S(1)} custom-call(f32[2,128,128]{2,1,0:T(8,128)} %get-tuple-element.246), custom_call_target="InvertDiagBlocksLowerTriangular" | custom-call | tf_op jit(solution)/shard_map/jit(_cho_solve)/triangular_solve | solution.py:38
  135.2 17.2 all-gather.2
  152.5 19.2 %all-gather.3 = bf16[16,16,6]{1,2,0:T(8,128)(2,1)S(1)} all-gather(bf16[1,16,6]{1,2,0:T(8,128)(2,1)S(1)} %convert_bitcast_fusion.2), channel_id=1, replica_groups=mesh['items'=16,'heads'=2] {'items'}, dimensions={0}, use_global_device_ids=true | all-gather | bytes 3264 | tf_op jit(solution)/shard_map/all_gather | solution.py:149
  171.8 20.7 %all_gather.99 = bf16[384,768]{0,1:T(8,128)(2,1)} all-gather(bf16[384,48]{0,1:T(8,128)(2,1)S(1)} %convert_element_type.415), channel_id=1, replica_groups=mesh['items'=16,'heads'=2] {'items'}, dimensions={1}, use_global_device_ids=true | all-gather | bytes 626688 | tf_op jit(solution)/shard_map/all_gather | solution.py:143
  217.6 108.6 %while.47 = (s32[]{:T(128)}, bf16[12,512,64]{1,2,0:T(8,128)(2,1)}, f32[12,512]{1,0:T(8,128)}, bf16[12,512,64]{2,1,0:T(8,128)(2,1)S(1)}, bf16[12,1024,64]{2,1,0:T...) while((s32[]{:T(128)}, bf16[12,512,64]{1,2,0:T(8,128)(2,1)}, ...), condition=%wide.region_23.26_spmd, body=%wide.region_20.25_spmd.sunk | while | flops 176200704 | bytes 9225857 | solution.py:204
  331.1 23.9 %reduce-scatter.21.cloned.1.call-done = bf16[1,512,768]{2,1,0:T(8,128)(2,1)} async-done(((bf16[2,512,768]{2,1,0:T(8,128)(2,1)}), bf16[1,512,768]{2,1,0:T(8,128)(2,1)}) %reduce-scatter.21.cloned.1.call-update) | async-done | bytes 786448 | tf_op jit(solution)/shard_map/reduce_scatter | solution.py:207
  360.2 40.2 %all-gather.43.cloned.1.call-done = bf16[768,1536]{1,0:T(8,128)(2,1)} async-done(((bf16[48,1536]{1,0:T(8,128)(2,1)}), bf16[768,1536]{1,0:T(8,128)(2,1)}) %all-gather.43.cloned.1.call-update) | async-done | bytes 2359312 | tf_op jit(solution)/shard_map/all_gather | solution.py:144
  400.4 28.1 %all-gather.41.cloned.1.call-done = bf16[2,512,768]{2,1,0:T(8,128)(2,1)} async-done(((bf16[1,512,768]{2,1,0:T(8,128)(2,1)}), bf16[2,512,768]{2,1,0:T(8,128)(2,1)}) %all-gather.41.cloned.1.call-update) | async-done | bytes 1572880 | tf_op jit(solution)/shard_map/all_gather | solution.py:211
  435.8 21.5 %all-gather.33.cloned.1.call-done = bf16[2,512,768]{2,1,0:T(8,128)(2,1)} async-done(((bf16[1,512,768]{2,1,0:T(8,128)(2,1)}), bf16[2,512,768]{2,1,0:T(8,128)(2,1)}) %all-gather.33.cloned.1.call-update) | async-done | bytes 1572880 | tf_op jit(solution)/shard_map/all_gather | solution.py:268
  457.3 45.5 %all-gather.31.cloned.1.call-done = bf16[1536,768]{0,1:T(8,128)(2,1)} async-done(((bf16[1536,48]{0,1:T(8,128)(2,1)}), bf16[1536,768]{0,1:T(8,128)(2,1)}) %all-gather.31.cloned.1.call-update) | async-done | bytes 2359312 | tf_op jit(solution)/shard_map/all_gather | solution.py:145
  517.2 25.0 %reduce-scatter.23.cloned.1.call-done = bf16[1,512,768]{2,1,0:T(8,128)(2,1)} async-done(((bf16[2,512,768]{2,1,0:T(8,128)(2,1)}), bf16[1,512,768]{2,1,0:T(8,128)(2,1)}) %reduce-scatter.23.cloned.1.call-update) | async-done | bytes 786448 | tf_op jit(solution)/shard_map/reduce_scatter | solution.py:277
  548.3 27.1 %all-gather.45.cloned.1.call-done = bf16[2,512,768]{2,1,0:T(8,128)(2,1)} async-done(((bf16[1,512,768]{2,1,0:T(8,128)(2,1)}), bf16[2,512,768]{2,1,0:T(8,128)(2,1)}) %all-gather.45.cloned.1.call-update) | async-done | bytes 1572880 | tf_op jit(solution)/shard_map/all_gather | solution.py:283
  580.3 267.8 %while.48 = (s32[]{:T(128)}, bf16[12,512,64]{1,2,0:T(8,128)(2,1)}, bf16[12,1024,64]{1,2,0:T(8,128)(2,1)}, bf16[12,1024,64]{1,2,0:T(8,128)(2,1)}, bf16[12,256,64]...) while((s32[]{:T(128)}, bf16[12,512,64]{1,2,0:T(8,128)(2,1)}, ...), condition=%wide.region_35.38_spmd, body=%wide.region_30.37_spmd.sunk | while | flops 436262400 | bytes 21539516 | solution.py:290
  882.0 18.1 %reduce-scatter.25.cloned.1.call-done = bf16[1,512,768]{2,1,0:T(8,128)(2,1)} async-done(((bf16[2,512,768]{2,1,0:T(8,128)(2,1)}), bf16[1,512,768]{2,1,0:T(8,128)(2,1)}) %reduce-scatter.25.cloned.1.call-update) | async-done | bytes 786448 | tf_op jit(solution)/shard_map/reduce_scatter | solution.py:319
  902.4 26.0 %reduce-scatter.35.cloned.1.call-done = bf16[1,512,768]{2,1,0:T(8,128)(2,1)} async-done(((bf16[2,512,768]{2,1,0:T(8,128)(2,1)}), bf16[1,512,768]{2,1,0:T(8,128)(2,1)}) %reduce-scatter.35.cloned.1.call-update) | async-done | bytes 786448 | tf_op jit(solution)/shard_map/reduce_scatter | solution.py:322
  934.8 21.5 %all-gather = bf16[16,16,6]{1,2,0:T(8,128)(2,1)S(1)} all-gather(bf16[1,16,6]{1,2,0:T(8,128)(2,1)S(1)} %convert_bitcast_fusion.5), channel_id=1, replica_groups=mesh['items'=16,'heads'=2] {'items'}, dimensions={0}, use_global_device_ids=true | all-gather | bytes 3264 | tf_op jit(solution)/shard_map/all_gather | solution.py:148
  957.7 17.5 all-gather.1
  982.6 21.8 %all_gather.85 = bf16[384,768]{0,1:T(8,128)(2,1)} all-gather(bf16[384,48]{0,1:T(8,128)(2,1)S(1)} %copy-done.35), channel_id=1, replica_groups=mesh['items'=16,'heads'=2] {'items'}, dimensions={1}, use_global_device_ids=true | all-gather | bytes 626688 | tf_op jit(solution)/shard_map/all_gather | solution.py:143
  1008.2 20.9 %all_gather.82 = bf16[2,256,768]{2,1,0:T(8,128)(2,1)S(1)} all-gather(bf16[1,256,768]{2,1,0:T(8,128)(2,1)S(1)} %copy.152), channel_id=1, replica_groups=mesh['items'=16,'heads'=2] {'heads'}, dimensions={0}, use_global_device_ids=true | all-gather | bytes 1179648 | tf_op jit(solution)/shard_map/all_gather | solution.py:183
  1056.5 102.3 %while.46 = (s32[]{:T(128)}, bf16[12,512,64]{1,2,0:T(8,128)(2,1)S(1)}, bf16[12,512,64]{2,1,0:T(8,128)(2,1)}, bf16[12,1024,64]{2,1,0:T(8,128)(2,1)}, bf16[12,1024...) while((s32[]{:T(128)}, ...), condition=%wide.region_11.14_spmd, body=%wide.region_8.13_spmd.sunk | while | flops 176200704 | bytes 9157221 | solution.py:204
  1164.3 20.2 %reduce-scatter.17.cloned.1.call-done = bf16[1,512,768]{2,1,0:T(8,128)(2,1)} async-done(((bf16[2,512,768]{2,1,0:T(8,128)(2,1)}), bf16[1,512,768]{2,1,0:T(8,128)(2,1)}) %reduce-scatter.17.cloned.1.call-update) | async-done | bytes 786448 | tf_op jit(solution)/shard_map/reduce_scatter | solution.py:207
  1212.8 16.7 all-gather.27.cloned.1.call-done
  1229.6 44.0 %all-gather.29.cloned.1.call-done = bf16[1536,768]{0,1:T(8,128)(2,1)} async-done(((bf16[1536,48]{0,1:T(8,128)(2,1)}), bf16[1536,768]{0,1:T(8,128)(2,1)}) %all-gather.29.cloned.1.call-update) | async-done | bytes 2359312 | tf_op jit(solution)/shard_map/all_gather | solution.py:145
  1273.6 27.4 %all-gather.25.cloned.1.call-done = bf16[2,512,768]{2,1,0:T(8,128)(2,1)} async-done(((bf16[1,512,768]{2,1,0:T(8,128)(2,1)}), bf16[2,512,768]{2,1,0:T(8,128)(2,1)}) %all-gather.25.cloned.1.call-update) | async-done | bytes 1572880 | tf_op jit(solution)/shard_map/all_gather | solution.py:211
  1330.4 29.1 %reduce-scatter.37.cloned.1.call-done = f32[16,6]{1,0:T(8,128)} async-done(((f32[256,6]{1,0:T(8,128)}), f32[16,6]{1,0:T(8,128)}) %reduce-scatter.37.cloned.1.call-update) | async-done | bytes 400
  1360.9 56.8 %reduce-scatter.39.cloned.1.call-done = f32[16,6]{1,0:T(8,128)} async-done(((f32[256,6]{1,0:T(8,128)}), f32[16,6]{1,0:T(8,128)}) %reduce-scatter.39.cloned.1.call-update) | async-done | bytes 400
  1421.8 115.6 %all-reduce.12.cloned.1.call-done = f32[3,768,384]{2,0,1:T(4,128)} async-done(((f32[3,768,384]{2,0,1:T(4,128)}), f32[3,768,384]{2,0,1:T(4,128)}) %all-reduce.12.cloned.1.call-update) | async-done | bytes 3538960
  1539.2 40.2 %all-reduce.8 = (f32[768]{0:T(1024)S(1)}, f32[768]{0:T(1024)S(1)}) all-reduce(f32[768]{0:T(1024)S(1)} %add.333, f32[768]{0:T(1024)S(1)} %copy-done.44), channel_id=13, replica_groups=mesh['items'=16,'heads'=2] {'items','heads'}, use_global_device_ids=true, to_apply=%region_47.50.clone | all-reduce | flops 1536 | bytes 12288
  1582.8 45.6 %reduce-scatter.29.cloned.1.call-done = f32[384,48]{0,1:T(8,128)} async-done(((f32[384,768]{0,1:T(8,128)}), f32[384,48]{0,1:T(8,128)}) %reduce-scatter.29.cloned.1.call-update) | async-done | bytes 73744 | tf_op jit(solution)/shard_map/reduce_scatter | solution.py:343
  1628.4 79.4 %reduce-scatter.31.cloned.1.call-done = f32[48,1536]{1,0:T(8,128)} async-done(((f32[768,1536]{1,0:T(8,128)}), f32[48,1536]{1,0:T(8,128)}) %reduce-scatter.31.cloned.1.call-update) | async-done | bytes 294928 | tf_op jit(solution)/shard_map/reduce_scatter | solution.py:344
  1707.8 79.0 %reduce-scatter.33.cloned.1.call-done = f32[1536,48]{0,1:T(8,128)} async-done(((f32[1536,768]{0,1:T(8,128)}), f32[1536,48]{0,1:T(8,128)}) %reduce-scatter.33.cloned.1.call-update) | async-done | bytes 294928 | tf_op jit(solution)/shard_map/reduce_scatter | solution.py:345
  (950 shorter events, 773.4 us)
Async XLA Ops:
  7.2 185.3 %all-gather.35.cloned.1.call-start = ((), (), s32[]{:S(2)}) async-start(), calls=%async_computation.22 | async-start | bytes 1880064 | tf_op jit(solution)/shard_map/all_gather | solution.py:142
  9.0 188.0 %all-gather.37.cloned.1.call-start = ((), (), s32[]{:S(2)}) async-start(), calls=%async_computation.23 | async-start | bytes 2359296 | tf_op jit(solution)/shard_map/all_gather | solution.py:181
  55.1 147.4 %all-gather.39.cloned.1.call-start = ((), (), s32[]{:S(2)}) async-start(), calls=%async_computation.24 | async-start | bytes 2359296 | tf_op jit(solution)/shard_map/all_gather | solution.py:182
  55.8 299.2 %reduce-scatter.21.cloned.1.call-start = ((), (), s32[]{:S(2)}) async-start(), calls=%async_computation.25 | async-start | bytes 2359296 | tf_op jit(solution)/shard_map/reduce_scatter | solution.py:207
  56.4 69.0 %copy-start.41 = (f32[256]{0:T(256)}, f32[256]{0:T(256)S(1)}, u32[]{:S(2)}) copy-start(f32[256]{0:T(256)S(1)} %add_multiply_fusion.5) | copy-start | bytes 3076
  330.3 70.1 %all-gather.43.cloned.1.call-start = ((), (), s32[]{:S(2)}) async-start(), calls=%async_computation.27 | async-start | bytes 2506752 | tf_op jit(solution)/shard_map/all_gather | solution.py:144
  331.0 97.4 %all-gather.41.cloned.1.call-start = ((), (), s32[]{:S(2)}) async-start(), calls=%async_computation.26 | async-start | bytes 2359296 | tf_op jit(solution)/shard_map/all_gather | solution.py:211
  358.2 99.1 %all-gather.33.cloned.1.call-start = ((), (), s32[]{:S(2)}) async-start(), calls=%async_computation.21 | async-start | bytes 2359296 | tf_op jit(solution)/shard_map/all_gather | solution.py:268
  359.0 143.8 %all-gather.31.cloned.1.call-start = ((), (), s32[]{:S(2)}) async-start(), calls=%async_computation.20 | async-start | bytes 2506752 | tf_op jit(solution)/shard_map/all_gather | solution.py:145
  359.7 182.5 %reduce-scatter.23.cloned.1.call-start = ((), (), s32[]{:S(2)}) async-start(), calls=%async_computation.28 | async-start | bytes 2359296 | tf_op jit(solution)/shard_map/reduce_scatter | solution.py:277
  517.2 58.2 %all-gather.45.cloned.1.call-start = ((), (), s32[]{:S(2)}) async-start(), calls=%async_computation.29 | async-start | bytes 2359296 | tf_op jit(solution)/shard_map/all_gather | solution.py:283
  548.1 330.6 %reduce-scatter.27.cloned.1.call-start = ((), (), s32[]{:S(2)}) async-start(), calls=%async_computation.31 | async-start | bytes 1179648 | tf_op jit(solution)/shard_map/reduce_scatter | solution.py:325
  853.6 46.5 %reduce-scatter.25.cloned.1.call-start = ((), (), s32[]{:S(2)}) async-start(), calls=%async_computation.30 | async-start | bytes 2359296 | tf_op jit(solution)/shard_map/reduce_scatter | solution.py:319
  869.1 59.3 %reduce-scatter.35.cloned.1.call-start = ((), (), s32[]{:S(2)}) async-start(), calls=%async_computation.35 | async-start | bytes 2359296 | tf_op jit(solution)/shard_map/reduce_scatter | solution.py:322
  874.4 154.6 %all-gather.21.cloned.1.call-start = ((), (), s32[]{:S(2)}) async-start(), calls=%async_computation.13 | async-start | bytes 1880064 | tf_op jit(solution)/shard_map/all_gather | solution.py:142
  876.2 156.9 %all-gather.19.cloned.1.call-start = ((), (), s32[]{:S(2)}) async-start(), calls=%async_computation.12 | async-start | bytes 2359296 | tf_op jit(solution)/shard_map/all_gather | solution.py:181
  932.6 105.6 %all-gather.23.cloned.1.call-start = ((), (), s32[]{:S(2)}) async-start(), calls=%async_computation.14 | async-start | bytes 2359296 | tf_op jit(solution)/shard_map/all_gather | solution.py:182
  1004.4 180.1 %reduce-scatter.17.cloned.1.call-start = ((), (), s32[]{:S(2)}) async-start(), calls=%async_computation.15 | async-start | bytes 2359296 | tf_op jit(solution)/shard_map/reduce_scatter | solution.py:207
  1162.1 67.5 %all-gather.27.cloned.1.call-start = ((), (), s32[]{:S(2)}) async-start(), calls=%async_computation.17 | async-start | bytes 2506752 | tf_op jit(solution)/shard_map/all_gather | solution.py:144
  1162.8 110.8 %all-gather.29.cloned.1.call-start = ((), (), s32[]{:S(2)}) async-start(), calls=%async_computation.18 | async-start | bytes 2506752 | tf_op jit(solution)/shard_map/all_gather | solution.py:145
  1163.7 137.3 %all-gather.25.cloned.1.call-start = ((), (), s32[]{:S(2)}) async-start(), calls=%async_computation.16 | async-start | bytes 2359296 | tf_op jit(solution)/shard_map/all_gather | solution.py:211
  1191.1 168.4 %reduce-scatter.37.cloned.1.call-start = ((), (), s32[]{:S(2)}) async-start(), calls=%async_computation.36 | async-start | bytes 139264
  1192.7 224.9 %reduce-scatter.39.cloned.1.call-start = ((), (), s32[]{:S(2)}) async-start(), calls=%async_computation.37 | async-start | bytes 139264
  1202.7 334.8 %all-reduce.12.cloned.1.call-start = ((), (), s32[]{:S(2)}) async-start(), calls=%async_computation.38 | async-start | bytes 9437184
  1212.8 367.7 %reduce-scatter.19.cloned.1.call-start = ((), (), s32[]{:S(2)}) async-start(), calls=%async_computation.19 | async-start | bytes 2359296 | tf_op jit(solution)/shard_map/reduce_scatter | solution.py:217
  1310.4 318.1 %reduce-scatter.29.cloned.1.call-start = ((), (), s32[]{:S(2)}) async-start(), calls=%async_computation.32 | async-start | bytes 1253376 | tf_op jit(solution)/shard_map/reduce_scatter | solution.py:343
  1314.3 393.5 %reduce-scatter.31.cloned.1.call-start = ((), (), s32[]{:S(2)}) async-start(), calls=%async_computation.33 | async-start | bytes 5013504 | tf_op jit(solution)/shard_map/reduce_scatter | solution.py:344
  1320.5 466.3 %reduce-scatter.33.cloned.1.call-start = ((), (), s32[]{:S(2)}) async-start(), calls=%async_computation.34 | async-start | bytes 5013504 | tf_op jit(solution)/shard_map/reduce_scatter | solution.py:345
  1329.8 89.3 %copy-start.42 = (f32[256]{0:T(256)S(1)}, f32[256]{0:T(256)}, u32[]{:S(2)}) copy-start(f32[256]{0:T(256)} %copy-done.41) | copy-start | bytes 3076
  1419.0 120.1 %copy-start.43 = (f32[768]{0:T(1024)S(1)}, f32[768]{0:T(1024)}, u32[]{:S(2)}) copy-start(f32[768]{0:T(1024)} %get-tuple-element.323) | copy-start | bytes 9220
  1419.0 120.1 %copy-start.48 = (f32[768]{0:T(1024)S(1)}, f32[768]{0:T(1024)}, u32[]{:S(2)}) copy-start(f32[768]{0:T(1024)} %get-tuple-element.450) | copy-start | bytes 9220
  1419.0 120.1 %copy-start.44 = (f32[768]{0:T(1024)S(1)}, f32[768]{0:T(1024)}, u32[]{:S(2)}) copy-start(f32[768]{0:T(1024)} %get-tuple-element.321) | copy-start | bytes 9220
  (52 other events, 395.4 us)
Sparse Core Ops, SparseCore 0:
  10.9 43.2 all-gather.34
  56.4 26.0 all-gather.36
  84.6 27.6 all-gather.38
  330.4 24.6 reduce-scatter.20
  358.0 42.3 all-gather.42
  402.4 25.9 all-gather.40
  430.0 27.2 all-gather.32
  460.4 42.3 all-gather.30
  517.3 24.8 reduce-scatter.22
  548.2 27.1 all-gather.44
  853.8 17.4 reduce-scatter.26
  874.0 26.0 reduce-scatter.24
  902.3 26.0 reduce-scatter.34
  931.5 40.6 all-gather.20
  973.6 26.0 all-gather.18
  1004.5 32.8 all-gather.22
  1162.2 22.3 reduce-scatter.16
  1187.2 42.3 all-gather.26
  1232.4 41.0 all-gather.28
  1275.0 25.9 all-gather.24
  1304.5 55.0 reduce-scatter.36
  1363.5 54.0 reduce-scatter.38
  1421.3 116.0 all-reduce.11
  1539.5 26.1 reduce-scatter.18
  1570.3 58.0 reduce-scatter.28
  1633.2 74.5 reduce-scatter.30
  1712.1 74.6 reduce-scatter.32
where the time goes:
time: 1810 us; the launch traced here: 1790 us
  waiting for transfers between devices  771 us (43%)
  matrix products  515 us (28%)
  blocking collectives  224 us (12%)
  local copies, waits for them, and re-layouts  136 us (8%)
  other arithmetic  125 us (7%)
  between operations  19.1 us (1%)
    unnamed x30, waiting for transfers between devices  203 us
    all_gather x2, waiting for transfers between devices, gather_weights(): lax.all_gather(w_down.astype(jnp.bfloat16), 'items', axis=1, tiled=True)  89.5 us
    reduce_scatter x1, waiting for transfers between devices, backward(): lax.psum_scatter(grad_w_up, 'items', scatter_dimension=0, tiled=True)  79.4 us
    reduce_scatter x1, waiting for transfers between devices, backward(): lax.psum_scatter(grad_w_down, 'items', scatter_dimension=1, tiled=True)  79 us
    unnamed x2, blocking collectives  76.5 us
    dot_general x36, matrix products, head_scores(): jnp.einsum('sd,td->st', queries, keys_all, preferred_element_type=jnp.flo...  61.1 us
    all_gather x2, waiting for transfers between devices, gather_weights(): lax.all_gather(w_up.astype(jnp.bfloat16), 'items', axis=0, tiled=True)  56.9 us
    all_gather x2, waiting for transfers between devices, forward(): normed_mlp = lax.all_gather(normed_mlp_own, 'heads', axis=0, tiled=True)  55.5 us
  transfers between devices with their start and end apart: 27, of which 19 were waited for; matrix products, arithmetic and copies ran while one was open for 12% of the time, Pallas kernels for 0%

commit v1 on v0

v1 whole, which is shorter than its diff:
```python
import math

import jax
import jax.numpy as jnp
import numpy as np
from jax import lax
from jax.experimental import pallas as pl
from jax.experimental.pallas import tpu as pltpu
from jax.sharding import PartitionSpec as P

HD = 64
GRID = 1024
EPSILON = 1e-05
VAR_SCALE = 0.01
RIDGE = 1.0
LANES = 128
ROWS = 256
NEG = -1e30
bf16 = jnp.bfloat16
f32 = jnp.float32


def dot(a, b, ca, cb):
    return lax.dot_general(a, b, (((ca,), (cb,)), ((), ())), preferred_element_type=f32)


def layer_norm(values, gain_vec):
    row_mean = jnp.mean(values, axis=-1, keepdims=True)
    centred = values - row_mean
    spread = jnp.mean(centred * centred, axis=-1, keepdims=True)
    return centred * lax.rsqrt(spread + EPSILON) * gain_vec


def basis_at(points, basis_count):
    centers = (jnp.arange(basis_count, dtype=f32) + 0.5) / basis_count
    offset = points[..., None] - centers
    return jnp.exp(-offset * offset * (0.5 * basis_count * basis_count))


def ridge_table(basis_count, samples):
    points = (np.arange(samples) + 0.5) / samples
    centers = (np.arange(basis_count) + 0.5) / basis_count
    design = np.exp(-((points[:, None] - centers) ** 2) * (0.5 * basis_count * basis_count))
    gram = design.T @ design + RIDGE * np.eye(basis_count)
    factor = np.linalg.cholesky(gram)
    table = np.linalg.solve(factor.T, np.linalg.solve(factor, design.T))
    return jnp.asarray(table.astype(np.float32)).astype(bf16)


def gelu_tanh(values):
    return jax.nn.gelu(values, approximate=True)


def near_scores(q_rows, keys, block):
    reach = keys.shape[0] // 2 + (block + 1) * ROWS
    scores = dot(q_rows, keys[:reach], 1, 1)
    row = lax.broadcasted_iota(jnp.int32, (ROWS, ROWS), 0)
    col = lax.broadcasted_iota(jnp.int32, (ROWS, ROWS), 1)
    edge = jnp.where(col <= row, scores[:, reach - ROWS :], NEG)
    return jnp.concatenate([scores[:, : reach - ROWS], edge], axis=1), reach


def density_parts(scaled, w_mean, w_var):
    basis_count = scaled.shape[1]
    index = lax.broadcasted_iota(jnp.int32, (1, basis_count), 1).astype(f32)
    centers = (index + 0.5) / basis_count
    middle = jax.nn.sigmoid(jnp.sum(scaled * w_mean, axis=1, keepdims=True))
    var_raw = jnp.sum(scaled * w_var, axis=1, keepdims=True)
    softplus = jnp.maximum(var_raw, 0.0) + jnp.log1p(jnp.exp(-jnp.abs(var_raw)))
    variance = VAR_SCALE * softplus + 1.0 / (basis_count * basis_count)
    offset = middle - centers
    inv_var = 1.0 / variance
    square = offset * offset * inv_var
    scale = lax.rsqrt(2.0 * math.pi * variance) / basis_count
    weights = jnp.exp(-0.5 * square) * scale
    return weights, middle, var_raw, inv_var, offset, square


def attn_fwd_kernel(q_ref, k_ref, v_ref, mk_ref, mv_ref, wm_ref, wv_ref, ctx_ref, lse_ref):
    half = lax.broadcasted_iota(jnp.int32, (1, LANES), 1) < HD
    length = q_ref.shape[0]
    keys, values = k_ref[...], v_ref[...]
    mem_keys, mem_values = mk_ref[...], mv_ref[...]
    for block in range(length // ROWS):
        rows = slice(block * ROWS, (block + 1) * ROWS)
        q_rows = q_ref[rows, :] * jnp.asarray(0.125, bf16)
        outs, sums = [], []
        for head in range(2):
            mine = half if head == 0 else jnp.logical_not(half)
            q_head = jnp.where(mine, q_rows, jnp.zeros_like(q_rows))
            scores, reach = near_scores(q_head, keys, block)
            top = jnp.max(scores, axis=1, keepdims=True)
            raw = jnp.exp(scores - top)
            total = jnp.sum(raw, axis=1, keepdims=True)
            probs = (raw * (1.0 / total)).astype(bf16)
            near = dot(probs, values[:reach], 1, 0)
            scaled = dot(q_head, mem_keys, 1, 1)
            weights = density_parts(
                scaled, wm_ref[0, head : head + 1, :], wv_ref[0, head : head + 1, :]
            )[0]
            outs.append(near + dot(weights.astype(bf16), mem_values, 1, 0))
            sums.append(top + jnp.log(total))
        ctx_ref[rows, :] = jnp.where(half, outs[0], outs[1]).astype(bf16)
        lse_ref[rows, :] = jnp.where(half, sums[0], sums[1])


def attn_bwd_kernel(
    q_ref, k_ref, v_ref, mk_ref, mv_ref, wm_ref, wv_ref, lse_ref, do_ref,
    dq_ref, dk_ref, dv_ref, gm_ref, gv_ref, acck_ref, accv_ref,
):
    half = lax.broadcasted_iota(jnp.int32, (1, LANES), 1) < HD
    length = q_ref.shape[0]
    near_rows = k_ref.shape[0]
    keys, values = k_ref[...], v_ref[...]
    mem_keys, mem_values = mk_ref[...], mv_ref[...]
    for block in reversed(range(length // ROWS)):
        rows = slice(block * ROWS, (block + 1) * ROWS)
        q_full, do_full = q_ref[rows, :], do_ref[rows, :]
        q_rows = q_full * jnp.asarray(0.125, bf16)
        q_turn, do_turn = q_full.T, do_full.T
        outs = []
        for head in range(2):
            part = slice(head * HD, (head + 1) * HD)
            mine = half if head == 0 else jnp.logical_not(half)
            q_head = jnp.where(mine, q_rows, jnp.zeros_like(q_rows))
            do_head = jnp.where(mine, do_full, jnp.zeros_like(do_full))
            scores, reach = near_scores(q_head, keys, block)
            probs = jnp.exp(scores - lse_ref[rows, head * HD : head * HD + 1])
            grad_probs = dot(do_head, values[:reach], 1, 1)
            inner = jnp.sum(probs * grad_probs, axis=1, keepdims=True)
            grad_raw = (0.125 * probs * (grad_probs - inner)).astype(bf16)
            probs_low = probs.astype(bf16)
            dk_part = dot(q_turn[part], grad_raw, 1, 0)
            dv_part = dot(do_turn[part], probs_low, 1, 0)
            out = dot(grad_raw, keys[:reach], 1, 0)
            w_mean, w_var = wm_ref[0, head : head + 1, :], wv_ref[0, head : head + 1, :]
            scaled = dot(q_head, mem_keys, 1, 1)
            weights, middle, var_raw, inv_var, offset, square = density_parts(scaled, w_mean, w_var)
            grad_w = dot(do_head, mem_values, 1, 1) * weights
            d_mid = -jnp.sum(grad_w * offset, axis=1, keepdims=True) * inv_var
            d_var = jnp.sum(grad_w * (square - 1.0), axis=1, keepdims=True) * (0.5 * inv_var)
            d_mid = d_mid * middle * (1.0 - middle)
            d_var = d_var * VAR_SCALE * jax.nn.sigmoid(var_raw)
            gm_part = jnp.sum(scaled * d_mid, axis=0, keepdims=True)
            gv_part = jnp.sum(scaled * d_var, axis=0, keepdims=True)
            grad_mem = (0.125 * (d_mid * w_mean + d_var * w_var)).astype(bf16)
            outs.append(out + dot(grad_mem, mem_keys, 1, 0))
            dmk_part = dot(q_turn[part], grad_mem, 1, 0)
            dmv_part = dot(do_turn[part], weights.astype(bf16), 1, 0)
            if block == length // ROWS - 1:
                acck_ref[part, :near_rows] = dk_part
                accv_ref[part, :near_rows] = dv_part
                acck_ref[part, near_rows:] = dmk_part
                accv_ref[part, near_rows:] = dmv_part
                gm_ref[0, head : head + 1, :] = gm_part
                gv_ref[0, head : head + 1, :] = gv_part
            else:
                acck_ref[part, :reach] += dk_part
                accv_ref[part, :reach] += dv_part
                acck_ref[part, near_rows:] += dmk_part
                accv_ref[part, near_rows:] += dmv_part
                gm_ref[0, head : head + 1, :] += gm_part
                gv_ref[0, head : head + 1, :] += gv_part
        dq_ref[rows, :] = jnp.where(half, outs[0], outs[1]).astype(bf16)
    dk_ref[...] = acck_ref[...].T.astype(bf16)
    dv_ref[...] = accv_ref[...].T.astype(bf16)


def attn_specs(length, basis_count, pairs, place):
    near_rows = 2 * length
    spec = pl.BlockSpec
    return [
        spec((length, LANES), lambda p: (0, place(p))),
        spec((near_rows, LANES), lambda p: (0, place(p))),
        spec((near_rows, LANES), lambda p: (0, pairs + place(p))),
        spec((basis_count, LANES), lambda p: (near_rows // basis_count, place(p))),
        spec((basis_count, LANES), lambda p: (near_rows // basis_count, pairs + place(p))),
        spec((1, 2, basis_count), lambda p: (place(p), 0, 0)),
        spec((1, 2, basis_count), lambda p: (place(p), 0, 0)),
    ]


def attn_forward(queries, kv, w_mean, w_var):
    length, width = queries.shape
    basis_count = w_mean.shape[-1]
    pairs = width // LANES
    return pl.pallas_call(
        attn_fwd_kernel,
        grid=(pairs,),
        in_specs=attn_specs(length, basis_count, pairs, lambda p: p),
        out_specs=[
            pl.BlockSpec((length, LANES), lambda p: (0, p)),
            pl.BlockSpec((length, LANES), lambda p: (0, p)),
        ],
        out_shape=[
            jax.ShapeDtypeStruct((length, width), bf16),
            jax.ShapeDtypeStruct((length, width), f32),
        ],
        compiler_params=pltpu.CompilerParams(vmem_limit_bytes=48 << 20),
        cost_estimate=pl.CostEstimate(
            flops=8 * length * length * width, bytes_accessed=8 << 20, transcendentals=0
        ),
        name="attn_forward",
    )(queries, kv, kv, kv, kv, w_mean, w_var)


def attn_backward(queries, kv, w_mean, w_var, lse, grad_ctx, group, groups):
    length, width = queries.shape
    basis_count = w_mean.shape[-1]
    pairs = width // LANES
    count = pairs // groups
    if groups == 1:
        place = lambda p: p
    else:
        place = lambda p: p * groups + group
    all_rows = kv.shape[0]
    out_width = count * LANES
    return pl.pallas_call(
        attn_bwd_kernel,
        grid=(count,),
        in_specs=attn_specs(length, basis_count, pairs, place)
        + [
            pl.BlockSpec((length, LANES), lambda p: (0, place(p))),
            pl.BlockSpec((length, LANES), lambda p: (0, place(p))),
        ],
        out_specs=[
            pl.BlockSpec((length, LANES), lambda p: (0, p)),
            pl.BlockSpec((all_rows, LANES), lambda p: (0, p)),
            pl.BlockSpec((all_rows, LANES), lambda p: (0, p)),
            pl.BlockSpec((1, 2, basis_count), lambda p: (p, 0, 0)),
            pl.BlockSpec((1, 2, basis_count), lambda p: (p, 0, 0)),
        ],
        out_shape=[
            jax.ShapeDtypeStruct((length, out_width), bf16),
            jax.ShapeDtypeStruct((all_rows, out_width), bf16),
            jax.ShapeDtypeStruct((all_rows, out_width), bf16),
            jax.ShapeDtypeStruct((count, 2, basis_count), f32),
            jax.ShapeDtypeStruct((count, 2, basis_count), f32),
        ],
        scratch_shapes=[
            pltpu.VMEM((LANES, all_rows), f32),
            pltpu.VMEM((LANES, all_rows), f32),
        ],
        compiler_params=pltpu.CompilerParams(vmem_limit_bytes=48 << 20),
        cost_estimate=pl.CostEstimate(
            flops=20 * length * length * out_width, bytes_accessed=8 << 20, transcendentals=0
        ),
        name="attn_backward",
    )(queries, kv, kv, kv, kv, w_mean, w_var, lse, grad_ctx)


class Links:
    def __init__(self, sizes):
        self.count = sizes["items"]
        self.bits = self.count.bit_length() - 1
        self.index = lax.axis_index("items")
        self.side = lax.axis_index("heads")

    def swap(self, value, stage):
        if stage == "h":
            return lax.ppermute(value, "heads", [(0, 1), (1, 0)])
        mask = 1 << stage
        return lax.ppermute(value, "items", [(i, i ^ mask) for i in range(self.count)])

    def bit(self, stage):
        return self.side if stage == "h" else (self.index >> stage) & 1

    def gather(self, value, lead, stages):
        have = []
        for stage in stages:
            other = self.swap(value, stage)
            mine_first = self.bit(stage) == 0
            first = jnp.where(mine_first, value, other)
            second = jnp.where(mine_first, other, value)
            if stage == "h":
                value = jnp.concatenate([first, second], axis=-1)
            else:
                place = sum(1 for b in have if b > stage)
                value = jnp.stack([first, second], axis=lead + place)
                have.append(stage)
        return value

    def reduce(self, value, lead, stages, wire):
        shape = value.shape
        value = value.reshape(shape[:lead] + (2,) * self.bits + shape[lead + 1 :])
        left = list(range(self.bits))[::-1]
        for stage in stages:
            bit = self.bit(stage)
            if stage == "h":
                width = value.shape[-1] // 2
                take = lambda b: lax.dynamic_slice_in_dim(value, b * width, width, axis=value.ndim - 1)
            else:
                axis = lead + left.index(stage)
                left.remove(stage)
                take = lambda b: lax.dynamic_index_in_dim(value, b, axis, keepdims=False)
            send = take(1 - bit).astype(wire)
            value = take(bit) + self.swap(send, stage).astype(f32)
        return value


def shards(
    tokens, earlier, coeffs, present, sample_at, w_qkv, w_out, w_up, w_down,
    gain_attn, gain_mlp, w_mean, w_var, cotangent, sizes, groups,
):
    links = Links(sizes)
    high = list(range(2, links.bits))
    count = links.count
    tokens, earlier, coeffs, cotangent = tokens[0], earlier[0], coeffs[0], cotangent[0]
    length, width = tokens.shape
    basis_count = coeffs.shape[0]
    rows, side = w_qkv.shape[1], w_qkv.shape[2]
    ff_side = w_up.shape[1]
    local_heads, mem_part = w_mean.shape

    small = jnp.concatenate(
        [gain_attn, gain_mlp, w_mean.reshape(-1), w_var.reshape(-1)]
    ).astype(bf16)
    small_size = small.shape[0]
    small = jnp.pad(small, (0, -small_size % LANES)).reshape(1, -1)
    small_h = links.swap(small, "h")
    first = jnp.where(links.side == 0, small, small_h)
    second = jnp.where(links.side == 0, small_h, small)
    small = links.gather(jnp.concatenate([first, second], axis=0), 0, high + [1, 0])
    small = small.reshape(count, 2, -1).astype(f32)
    gain_a = small[:, 0, :rows].reshape(-1)
    gain_m = small[:, 0, rows : 2 * rows].reshape(-1)

    def head_map(start):
        part = small[:, :, start : start + local_heads * mem_part]
        part = part.reshape(count, 2, local_heads, mem_part).transpose(1, 2, 0, 3)
        return part.reshape(local_heads, 2, basis_count)

    mean_full = head_map(2 * rows)
    var_full = head_map(2 * rows + local_heads * mem_part)

    qkv_full = links.gather(w_qkv.astype(bf16), 1, high + [1, "h", 0])
    qkv_full = qkv_full.reshape(3, width, width)
    rest = jnp.concatenate([w_out.T, w_up, w_down.T], axis=1).astype(bf16)
    rest = lax.all_gather(rest, ("items", "heads"), axis=0, tiled=False)
    rest = rest.reshape(count, 2, rows, -1)

    def whole(start, size):
        return rest[..., start : start + size].transpose(0, 2, 1, 3).reshape(width, 2 * size)

    out_turn = whole(0, side)
    up_full = whole(side, ff_side)
    down_turn = whole(side + ff_side, ff_side)

    ridge = ridge_table(basis_count, 2 * length)
    tokens32, earlier32 = tokens.astype(f32), earlier.astype(f32)
    normed = layer_norm(tokens32, gain_a).astype(bf16)
    past = layer_norm(earlier32, gain_a).astype(bf16)
    old_basis = basis_at((sample_at[0].astype(f32) + 0.5) / GRID, basis_count).astype(bf16)
    here = present[0].astype(f32)
    samples = (here * dot(old_basis, coeffs.astype(bf16), 1, 0)).astype(bf16)
    memory = dot(ridge, jnp.concatenate([samples, past], axis=0), 1, 0).astype(bf16)
    sources = jnp.concatenate([past, normed, memory], axis=0)
    queries = dot(normed, qkv_full[0], 1, 0).astype(bf16)
    kv = jnp.concatenate(
        [dot(sources, qkv_full[1], 1, 0), dot(sources, qkv_full[2], 1, 0)], axis=1
    ).astype(bf16)
    context, lse = attn_forward(queries, kv, mean_full, var_full)
    hidden = tokens32 + dot(context, out_turn, 1, 1)
    normed_mlp, mlp_pull = jax.vjp(layer_norm, hidden, gain_m)
    normed_mlp = normed_mlp.astype(bf16)
    pre_act = dot(normed_mlp, up_full, 1, 0)
    activation = gelu_tanh(pre_act).astype(bf16)
    output = (hidden + dot(activation, down_turn, 1, 1)).astype(bf16)

    grad_act = dot(cotangent, down_turn, 1, 0)
    _, gelu_pull = jax.vjp(gelu_tanh, pre_act)
    grad_pre = gelu_pull(grad_act)[0].astype(bf16)
    g_down = dot(cotangent, activation, 0, 0).reshape(count, rows, -1)
    g_up = dot(normed_mlp, grad_pre, 0, 0).reshape(count, rows, -1)
    down = high[::-1]
    r_down = links.reduce(g_down, 0, [0, "h", 1] + down, bf16)
    r_up = links.reduce(g_up, 0, [0, 1, "h"] + down, bf16)
    grad_hidden_norm, gain_m_grad = mlp_pull(dot(grad_pre, up_full, 1, 1))
    grad_hidden = cotangent.astype(f32) + grad_hidden_norm
    grad_branch = grad_hidden.astype(bf16)
    g_out = dot(grad_branch, context, 0, 0).reshape(count, rows, -1)
    r_out = links.reduce(g_out, 0, [0, 1, "h"] + down, bf16)
    grad_ctx = dot(grad_branch, out_turn, 1, 0).astype(bf16)

    grad_sources = 0.0
    grad_normed = 0.0
    r_qkv, mean_grads, var_grads = [], [], []
    pairs = width // LANES
    for group in range(groups):
        dq, dk, dv, gm, gv = attn_backward(
            queries, kv, mean_full, var_full, lse, grad_ctx, group, groups
        )
        grads = [dot(normed, dq, 0, 0), dot(sources, dk, 0, 0), dot(sources, dv, 0, 0)]
        g_qkv = jnp.stack(grads).reshape(3, count, rows, -1)
        order = [0, "h", 1] if group % 2 == 0 else [0, 1, "h"]
        r_qkv.append(links.reduce(g_qkv, 1, order + down, bf16))
        mean_grads.append(gm)
        var_grads.append(gv)
        part = qkv_full.reshape(3, width, pairs // groups, groups, LANES)[:, :, :, group]
        part = part.reshape(3, width, -1)
        grad_normed = grad_normed + dot(dq, part[0], 1, 1)
        grad_sources = grad_sources + dot(dk, part[1], 1, 1) + dot(dv, part[2], 1, 1)
    grad_normed = grad_normed + grad_sources[length : 2 * length]
    grad_memory = grad_sources[2 * length :].astype(bf16)
    grad_fit = dot(ridge, grad_memory, 0, 0)
    grad_samples = grad_fit[:length].astype(bf16)
    grad_coeffs = here * dot(old_basis, grad_samples, 0, 0)
    grad_past = grad_sources[:length] + grad_fit[length:]
    _, first_pull = jax.vjp(layer_norm, tokens32, gain_a)
    grad_tokens_norm, gain_one = first_pull(grad_normed)
    _, past_pull = jax.vjp(layer_norm, earlier32, gain_a)
    _, gain_two = past_pull(grad_past)
    grad_tokens = grad_hidden + grad_tokens_norm

    def by_owner(gain):
        return gain.reshape(count, 2, -1)

    def map_owner(parts):
        full = jnp.stack(parts, axis=1).reshape(2, local_heads, count, mem_part)
        return full.transpose(2, 0, 1, 3).reshape(count, 2, -1)

    tiny = jnp.concatenate(
        [by_owner(gain_one + gain_two), by_owner(gain_m_grad), map_owner(mean_grads), map_owner(var_grads)],
        axis=2,
    )
    gain_part = width // (2 * count)
    map_part = local_heads * mem_part
    tiny = jnp.pad(tiny, ((0, 0), (0, 0), (0, -tiny.shape[2] % LANES)))
    tiny = links.reduce(tiny.reshape(count, 1, -1), 0, [0, "h", 1] + down, f32).reshape(-1)
    gain_a_out = tiny[:gain_part]
    gain_m_out = tiny[gain_part : 2 * gain_part]
    mean_out = tiny[2 * gain_part : 2 * gain_part + map_part].reshape(local_heads, mem_part)
    var_out = tiny[2 * gain_part + map_part : 2 * gain_part + 2 * map_part]
    var_out = var_out.reshape(local_heads, mem_part)
    return (
        output[None],
        grad_tokens[None],
        grad_coeffs[None],
        jnp.concatenate(r_qkv, axis=2),
        r_out.T,
        r_up,
        r_down.T,
        gain_a_out,
        gain_m_out,
        mean_out,
        var_out,
    )


def solution(mesh):
    sizes = dict(mesh.shape)
    both = ("items", "heads")
    in_specs = (
        P(both, None, None),
        P(both, None, None),
        P(both, None, None),
        P(both),
        P(both, None),
        P(None, "items", "heads"),
        P("heads", "items"),
        P("items", "heads"),
        P("heads", "items"),
        P("items"),
        P("items"),
        P("heads", "items"),
        P("heads", "items"),
        P(both, None, None),
    )
    out_specs = (
        P(both, None, None),
        P(both, None, None),
        P(both, None, None),
        P(None, "items", "heads"),
        P("heads", "items"),
        P("items", "heads"),
        P("heads", "items"),
        P(both),
        P(both),
        P("heads", "items"),
        P("heads", "items"),
    )

    def body(*args):
        return shards(*args, sizes=sizes, groups=3)

    return jax.shard_map(body, mesh=mesh, in_specs=in_specs, out_specs=out_specs, check_vma=False)
```

time: 1810 us -> 478 us (0.26)
  waiting for transfers between devices: 771 us -> 133 us
  matrix products: 515 us -> 61.2 us
  blocking collectives: 224 us -> 0 us
  other arithmetic: 125 us -> 35.6 us
  Pallas kernels: 0 us -> 58.4 us
  starting transfers between devices: 2.61 us -> 48.2 us
    dot_general x341 -> x34, matrix products: 511 us -> 61.2 us  [dot(): lax.dot_general(a, b, (((ca,), (cb,)), ((), ())), preferred_element_type=...]
    reduce_scatter x10 -> x0, waiting for transfers between devices: 317 us -> none  [the longest x1 79.4 us: backward(): lax.psum_scatter(grad_w_up, 'items', scatter_dimension=0, tiled=True)]
    all_gather x14 -> x1, waiting for transfers between devices: 250 us -> 0.02 us  [shards(): rest = lax.all_gather(rest, ('items', 'heads'), axis=0, tiled=False)]
    unnamed x30 -> x1, waiting for transfers between devices: 203 us -> 0.02 us
    all_gather x8 -> x0, blocking collectives: 147 us -> none  [the longest x2 42.5 us: gather_weights(): lax.all_gather(w_out.astype(jnp.bfloat16), 'items', axis=1, tiled=True)]
    ppermute x0 -> x45, waiting for transfers between devices: none -> 133 us  [the longest x36 87.2 us: swap(): lax.ppermute(value, 'items', [(i, i ^ mask) for i in range(self.count)])]
    unnamed x2 -> x0, blocking collectives: 76.5 us -> none
    pallas_call x0 -> x4, Pallas kernels: none -> 58.4 us  [the longest x3 38.5 us: attn_backward(): pl.pallas_call(attn_bwd_kernel, grid=(count,), in_specs=attn_specs(length...]
  transfers between devices with their start and end apart: 27 -> 46, of which waited for: 19 -> 26; matrix products, arithmetic and copies ran while one was open for 12% -> 22% of each run, Pallas kernels for 0% -> 4%
where the time goes in v1:
time: 478 us; the launch traced here: 472 us
  waiting for transfers between devices  133 us (28%)
  local copies, waits for them, and re-layouts  119 us (25%)
  matrix products  61.2 us (13%)
  Pallas kernels  58.4 us (12%)
  starting transfers between devices  48.2 us (10%)
  other arithmetic  35.6 us (7%)
  between operations  16.6 us (3%)
    ppermute x36, waiting for transfers between devices, swap(): lax.ppermute(value, 'items', [(i, i ^ mask) for i in range(self.count)])  87.2 us
    dot_general x34, matrix products, dot(): lax.dot_general(a, b, (((ca,), (cb,)), ((), ())), preferred_element_type=...  61.2 us
    ppermute x9, waiting for transfers between devices, swap(): return lax.ppermute(value, 'heads', [(0, 1), (1, 0)])  45.6 us
    unnamed x143, local copies, waits for them, and re-layouts  42.4 us
    ppermute x36, starting transfers between devices, swap(): lax.ppermute(value, 'items', [(i, i ^ mask) for i in range(self.count)])  40.4 us
    pallas_call x3, Pallas kernels, attn_backward(): pl.pallas_call(attn_bwd_kernel, grid=(count,), in_specs=attn_specs(length...  38.5 us
    slice x4, local copies, waits for them, and re-layouts, shards(): grad_normed = grad_normed + dot(dq, part[0], 1, 1)  20.3 us
    pallas_call x1, Pallas kernels, attn_forward(): pl.pallas_call(attn_fwd_kernel, grid=(pairs,), in_specs=attn_specs(length...  19.9 us
  transfers between devices with their start and end apart: 46, of which 26 were waited for; matrix products, arithmetic and copies ran while one was open for 22% of the time, Pallas kernels for 4%

profile of v1, /device:TPU:0, one launch (start us, length us, event | category | flops | bytes accessed | tf_op | source)
XLA Modules:
  0.0 471.9 jit_solution(10968409633936595241)
XLA Ops:
  11.4 3.0 collective-permute-start
  23.7 13.3 %collective-permute-done.6 = bf16[3,2,48,384]{3,2,1,0:T(8,128)(2,1)S(1)} collective-permute-done((bf16[3,2,48,384]{3,2,1,0:T(8,128)(2,1)S(1)}, bf16[3,2,48,384]{3,2,1,0:T(8,128)(2,1)S(1)}, u32[]{:S(2)}, u32[]{:S(2)}) %collective-permute-start.6) | collective-permute-done | bytes 221216 | tf_op jit(solution)/shard_map/ppermute | solution.py:263
  38.8 10.8 %collective-permute-done.7 = bf16[3,2,2,48,384]{4,3,2,1,0:T(8,128)(2,1)S(1)} collective-permute-done((bf16[3,2,2,48,384]{4,3,2,1,0:T(8,128)(2,1)S(1)}, bf16[3,2,2,48,384]{4,3,2,1,0:T(8,128)(2,1)S(1)}, u32[]{:S(2)}, u32[]{:S(2)}) %collective-permute-start.7) | collective-permute-done | bytes 442400 | tf_op jit(solution)/shard_map/ppermute | solution.py:263
  54.4 14.9 %collective-permute-done.8 = bf16[3,2,2,2,48,384]{5,4,3,2,1,0:T(8,128)(2,1)S(1)} collective-permute-done((bf16[3,2,2,2,48,384]{5,4,3,2,1,0:T(8,128)(2,1)S(1)}, bf16[3,2,2,2,48,384]{5,4,3,2,1,0:T(8,128)(2,1)S(1)}, u32[]{:S(2)}, u32[]{:S(2)}) %collective-permute-start.8) | collective-permute-done | bytes 884768 | tf_op jit(solution)/shard_map/ppermute | solution.py:261
  86.4 9.2 %reshape_reshape.20 = bf16[3,768,2,3,128]{4,3,2,1,0:T(4,128)(2,1)} reshape(bf16[3,2,2,2,2,48,768]{6,5,4,3,2,1,0:T(8,128)(2,1)} %pad_maximum_fusion) | data formatting | bytes 7077888 | tf_op jit(solution)/shard_map/reshape;reshape | solution.py:399
  95.6 12.9 %fusion.138 = (bf16[1,768,2,1,128]{4,3,2,1,0:T(2,128)(2,1)}, bf16[1,768,2,1,128]{4,3,2,1,0:T(2,128)(2,1)}, bf16[1,768,2,1,128]{4,3,2,1,0:T(2,128)(2,1)}, bf16[1,...) fusion(bf16[3,768,2,3,128]{4,3,2,1,0:T(4,128)(2,1)} %reshape_re, ...), kind=kLoop, calls=%fused_computation.314 | loop fusion | bytes 7077888 | tf_op jit(solution)/shard_map/slice | solution.py:401
  141.9 19.9 %attn_forward.1 = (bf16[512,768]{1,0:T(8,128)(2,1)S(1)}, f32[512,768]{1,0:T(8,128)S(1)}) custom-call(bf16[512,768]{1,0:T(8,128)(2,1)S(1)} %convolution_convert_fusion.3.q_ref, bf16[1280,1536]{1,0:T(8,128)(2,1)} %pad_maximum_fusion.1.k_ref.v_ref.mk_ref.mv_ref, bf16[1280,1536]{1,0:T(8,128)(2,1)} %pad_maximum_fusion.1.k_ref.v_ref.mk_ref.mv_ref, ...), custom_call_target="tpu_custom_call" | custom-call | flops 1610612736 | bytes 8388608 | tf_op jit(solution)/shard_map/attn_forward/pallas_call | solution.py:187
  164.2 8.4 %fusion.137 = (bf16[16,2,48,1536]{3,2,1,0:T(8,128)(2,1)}, bf16[16,2,48,1536]{3,2,1,0:T(8,128)(2,1)}) fusion(bf16[16,2,48,3456]{3,2,1,0:T(8,128)(2,1)} %bitcast.421), kind=kLoop, calls=%fused_computation.313 | loop fusion | bytes 18874368 | tf_op jit(solution)/shard_map/slice | solution.py:343
  172.6 9.4 %copy.183 = bf16[16,2,48,1536]{3,1,2,0:T(2,128)(2,1)} copy(bf16[16,2,48,1536]{3,2,1,0:T(8,128)(2,1)} %get-tuple-element.55) | data formatting | bytes 9437184
  182.0 5.7 %copy.190 = bf16[96,8,2,1536]{3,1,2,0:T(8,128)(2,1)} copy(bf16[96,8,2,1536]{3,2,1,0:T(2,128)(2,1)} %bitcast.413) | data formatting | bytes 9437184
  191.4 9.6 %copy.184 = bf16[16,2,48,1536]{3,1,2,0:T(2,128)(2,1)} copy(bf16[16,2,48,1536]{3,2,1,0:T(8,128)(2,1)} %get-tuple-element.56) | data formatting | bytes 9437184
  201.0 3.6 copy.191
  204.6 4.6 fusion.129
  209.3 4.8 %fusion.36 = bf16[1,512,768]{2,1,0:T(8,128)(2,1)} fusion(f32[512,768]{1,0:T(8,128)S(1)} %copy-done.8, bf16[768,3072]{1,0:T(8,128)(2,1)S(1)} %bitcast.428, f32[512,3072]{1,0:T(8,128)S(1)} %fusion.129), kind=kOutput, calls=%fused_computation.91 | convolution fusion | flops 2430861312 | bytes 13369344 | tf_op jit(solution)/shard_map/dot_general | solution.py:24
  214.1 6.5 %fusion.6 = bf16[512,3072]{1,0:T(8,128)(2,1)S(1)} fusion(f32[512,3072]{1,0:T(8,128)S(1)} %fusion.129, bf16[768,3072]{1,0:T(8,128)(2,1)S(1)} %bitcast.429, bf16[1,512,768]{2,1,0:T(8,128)(2,1)S(1)} %copy-done.22), kind=kOutput, calls=%fused_computation.8 | convolution fusion | flops 2447376384 | bytes 14942208 | tf_op jit(solution)/shard_map/dot_general | solution.py:24
  229.2 12.6 %attn_backward.5 = (bf16[512,256]{1,0:T(8,128)(2,1)S(1)}, bf16[1280,256]{1,0:T(8,128)(2,1)S(1)}, bf16[1280,256]{1,0:T(8,128)(2,1)S(1)}, f32[2,2,256]{2,1,0:T(2,128)S(1)}, f32[2,2,256]{2,1,0:T(2,128)S(1)}) custom-call(bf16[512,768]{1,0:T(8,128)(2,1)S(1)} %convolution_convert_fusion.3.q_ref, bf16[1280,1536]{1,0:T(8,128)(2,1)} %pad_maximum_fusion.1.k_ref.v_ref.mk_ref.mv_ref, ...), custom_call_target="tpu_custom_call" | custom-call | flops 1342177280 | bytes 8388608 | tf_op jit(solution)/shard_map/attn_backward/pallas_call | solution.py:218
  241.8 12.8 %attn_backward.4 = (bf16[512,256]{1,0:T(8,128)(2,1)S(1)}, bf16[1280,256]{1,0:T(8,128)(2,1)S(1)}, bf16[1280,256]{1,0:T(8,128)(2,1)S(1)}, f32[2,2,256]{2,1,0:T(2,128)S(1)}, f32[2,2,256]{2,1,0:T(2,128)S(1)}) custom-call(bf16[512,768]{1,0:T(8,128)(2,1)S(1)} %convolution_convert_fusion.3.q_ref, bf16[1280,1536]{1,0:T(8,128)(2,1)} %pad_maximum_fusion.1.k_ref.v_ref.mk_ref.mv_ref, ...), custom_call_target="tpu_custom_call" | custom-call | flops 1342177280 | bytes 8388608 | tf_op jit(solution)/shard_map/attn_backward/pallas_call | solution.py:218
  254.6 13.1 %attn_backward.3 = (bf16[512,256]{1,0:T(8,128)(2,1)S(1)}, bf16[1280,256]{1,0:T(8,128)(2,1)S(1)}, bf16[1280,256]{1,0:T(8,128)(2,1)S(1)}, f32[2,2,256]{2,1,0:T(2,128)S(1)}, f32[2,2,256]{2,1,0:T(2,128)S(1)}) custom-call(bf16[512,768]{1,0:T(8,128)(2,1)S(1)} %convolution_convert_fusion.3.q_ref, bf16[1280,1536]{1,0:T(8,128)(2,1)} %pad_maximum_fusion.1.k_ref.v_ref.mk_ref.mv_ref, ...), custom_call_target="tpu_custom_call" | custom-call | flops 1342177280 | bytes 8388608 | tf_op jit(solution)/shard_map/attn_backward/pallas_call | solution.py:218
  287.1 5.4 %fusion.48 = f32[3072,768]{0,1:T(8,128)} fusion(bf16[1,512,768]{2,1,0:T(8,128)(2,1)S(1)} %copy-done.23, f32[512,3072]{1,0:T(8,128)S(1)} %bitcast.459), kind=kOutput, calls=%fused_computation.122 | convolution fusion | flops 2430074880 | bytes 16515072 | tf_op jit(solution)/shard_map/dot_general | solution.py:24
  292.5 5.7 %fusion.128 = f32[768,3072]{1,0:T(8,128)} fusion(bf16[512,3072]{1,0:T(8,128)(2,1)S(1)} %copy-done.31, f32[512,768]{1,0:T(8,128)S(1)} %copy-done.8, f32[768]{0:T(1024)S(1)} %mul.270, f32[512]{0:T(512)S(1)} %fusion.115, f32[512]{0:T(512)S(1)} %broadcast_multiply_fusion), kind=kOutput, calls=%fused_computation.304 | convolution fusion | flops 2417491968 | bytes 14162944 | tf_op jit(solution)/shard_map/dot_general | solution.py:24
  311.0 4.3 fusion.10
  326.6 4.3 collective-permute-done.43
  330.9 7.7 %collective-permute-start.44 = (f32[1,256]{1,0:T(1,128)S(1)}, f32[1,256]{1,0:T(1,128)S(1)}, u32[]{:S(2)}, u32[]{:S(2)}) collective-permute-start(f32[1,256]{1,0:T(1,128)S(1)} %fusion.123), channel_id=1, source_target_pairs={{0,8},{2,10},{4,12},{6,14},{8,0},{10,2},{12,4},{14,6},{16,24},{18,... | collective-permute-start | bytes 3080 | tf_op jit(solution)/shard_map/ppermute | solution.py:263
  338.6 4.1 fusion.11
  352.0 4.3 collective-permute-done.26
  366.4 3.0 collective-permute-done.27
  389.7 3.8 bitcast_add_fusion
  397.5 20.3 %collective-permute-done.36 = bf16[2,2,2,48,1536]{4,3,1,0,2:T(8,128)(2,1)S(1)} collective-permute-done((bf16[2,2,2,48,1536]{4,3,1,0,2:T(8,128)(2,1)S(1)}, bf16[2,2,2,48,1536]{4,3,1,0,2:T(8,128)(2,1)S(1)}, u32[]{:S(2)}, u32[]{:S(2)}) %collective-permute-start.36) | collective-permute-done | bytes 1179680 | tf_op jit(solution)/shard_map/ppermute | solution.py:261
  422.2 3.1 collective-permute-start.32
  425.2 6.4 %collective-permute-done.37 = bf16[2,2,48,1536]{3,2,1,0:T(8,128)(2,1)S(1)} collective-permute-done((bf16[2,2,48,1536]{3,2,1,0:T(8,128)(2,1)S(1)}, bf16[2,2,48,1536]{3,2,1,0:T(8,128)(2,1)S(1)}, u32[]{:S(2)}, u32[]{:S(2)}) %collective-permute-start.37) | collective-permute-done | bytes 589856 | tf_op jit(solution)/shard_map/ppermute | solution.py:263
  435.1 16.9 %collective-permute-done.38 = bf16[2,48,1536]{2,1,0:T(8,128)(2,1)S(1)} collective-permute-done((bf16[2,48,1536]{2,1,0:T(8,128)(2,1)S(1)}, bf16[2,48,1536]{2,1,0:T(8,128)(2,1)S(1)}, u32[]{:S(2)}, u32[]{:S(2)}) %collective-permute-start.38) | collective-permute-done | bytes 294944 | tf_op jit(solution)/shard_map/ppermute | solution.py:263
  452.2 5.8 %collective-permute-done.33 = bf16[2,48,1536]{2,1,0:T(8,128)(2,1)S(1)} collective-permute-done((bf16[2,48,1536]{2,1,0:T(8,128)(2,1)S(1)}, bf16[2,48,1536]{2,1,0:T(8,128)(2,1)S(1)}, u32[]{:S(2)}, u32[]{:S(2)}) %collective-permute-start.33) | collective-permute-done | bytes 294944 | tf_op jit(solution)/shard_map/ppermute | solution.py:263
  (425 shorter events, 185.0 us)
Async XLA Ops:
  7.3 154.6 %all-gather.2.cloned.1.call-start = ((), (), s32[]{:S(2)}) async-start(), calls=%async_computation | async-start | bytes 10948608 | tf_op jit(solution)/shard_map/all_gather | solution.py:339
  11.4 10.6 %collective-permute-start = (bf16[1,384]{1,0:T(2,128)(2,1)S(1)}, bf16[1,384]{1,0:T(2,128)(2,1)S(1)}, u32[]{:S(2)}, u32[]{:S(2)}) collective-permute-start(bf16[1,384]{1,0:T(2,128)(2,1)S(1)} %reshape.334), channel_id=1, source_target_pairs={{0,1},{1,0},{2,3},{3,2},{4,5},{5,4},{6,7},{7,6},{8,9},{9,8},{10,11... | collective-permute-start | bytes 2312 | tf_op jit(solution)/shard_map/ppermute | solution.py:261
  19.4 17.7 %collective-permute-start.6 = (bf16[3,2,48,384]{3,2,1,0:T(8,128)(2,1)S(1)}, bf16[3,2,48,384]{3,2,1,0:T(8,128)(2,1)S(1)}, u32[]{:S(2)}, u32[]{:S(2)}) collective-permute-start(bf16[3,2,48,384]{3,2,1,0:T(8,128)(2,1)S(1)} %pad_maximum_fusion.10), channel_id=1, source_target_pairs={{0,16},{2,18},{4,20},{6,22},{8,24},{10,26},{12,28},{14,30},{16,0},... | collective-permute-start | bytes 663560 | tf_op jit(solution)/shard_map/ppermute | solution.py:263
  22.0 16.7 %collective-permute-start.1 = (bf16[2,384]{1,0:T(2,128)(2,1)S(1)}, bf16[2,384]{1,0:T(2,128)(2,1)S(1)}, u32[]{:S(2)}, u32[]{:S(2)}) collective-permute-start(bf16[2,384]{1,0:T(2,128)(2,1)S(1)} %pad_maximum_fusion.19), channel_id=1, source_target_pairs={{0,8},{2,10},{4,12},{6,14},{8,0},{10,2},{12,4},{14,6},{16,24},{18,... | collective-permute-start | bytes 4616 | tf_op jit(solution)/shard_map/ppermute | solution.py:263
  37.2 12.5 %collective-permute-start.7 = (bf16[3,2,2,48,384]{4,3,2,1,0:T(8,128)(2,1)S(1)}, bf16[3,2,2,48,384]{4,3,2,1,0:T(8,128)(2,1)S(1)}, u32[]{:S(2)}, u32[]{:S(2)}) collective-permute-start(bf16[3,2,2,48,384]{4,3,2,1,0:T(8,128)(2,1)S(1)} %pad_maximum_fusion.8), channel_id=1, source_target_pairs={{0,4},{2,6},{4,0},{6,2},{8,12},{10,14},{12,8},{14,10},{16,20},{18,... | collective-permute-start | bytes 1327112 | tf_op jit(solution)/shard_map/ppermute | solution.py:263
  38.8 11.2 %collective-permute-start.2 = (bf16[2,2,384]{2,1,0:T(2,128)(2,1)S(1)}, bf16[2,2,384]{2,1,0:T(2,128)(2,1)S(1)}, u32[]{:S(2)}, u32[]{:S(2)}) collective-permute-start(bf16[2,2,384]{2,1,0:T(2,128)(2,1)S(1)} %pad_maximum_fusion.18), channel_id=1, source_target_pairs={{0,16},{2,18},{4,20},{6,22},{8,24},{10,26},{12,28},{14,30},{16,0},... | collective-permute-start | bytes 9224 | tf_op jit(solution)/shard_map/ppermute | solution.py:263
  49.9 19.4 %collective-permute-start.8 = (bf16[3,2,2,2,48,384]{5,4,3,2,1,0:T(8,128)(2,1)S(1)}, bf16[3,2,2,2,48,384]{5,4,3,2,1,0:T(8,128)(2,1)S(1)}, u32[]{:S(2)}, u32[]{:S(2)}) collective-permute-start(bf16[3,2,2,2,48,384]{5,4,3,2,1,0:T(8,128)(2,1)S(1)} %pad_maximum_fusion.7), channel_id=1, source_target_pairs={{0,1},{1,0},{2,3},{3,2},{4,5},{5,4},{6,7},{7,6},{8,9},{9,8},{10,11... | collective-permute-start | bytes 2654216 | tf_op jit(solution)/shard_map/ppermute | solution.py:261
  54.3 17.5 %collective-permute-start.4 = (bf16[2,2,2,2,384]{4,3,2,1,0:T(2,128)(2,1)S(1)}, bf16[2,2,2,2,384]{4,3,2,1,0:T(2,128)(2,1)S(1)}, u32[]{:S(2)}, u32[]{:S(2)}) collective-permute-start(bf16[2,2,2,2,384]{4,3,2,1,0:T(2,128)(2,1)S(1)} %pad_maximum_fusion.14), channel_id=1, source_target_pairs={{0,2},{2,0},{4,6},{6,4},{8,10},{10,8},{12,14},{14,12},{16,18},{18,... | collective-permute-start | bytes 36872 | tf_op jit(solution)/shard_map/ppermute | solution.py:263
  71.1 9.6 %collective-permute-start.9 = (bf16[3,2,2,2,48,768]{5,4,3,2,1,0:T(8,128)(2,1)}, bf16[3,2,2,2,48,768]{5,4,3,2,1,0:T(8,128)(2,1)}, u32[]{:S(2)}, u32[]{:S(2)}) collective-permute-start(bf16[3,2,2,2,48,768]{5,4,3,2,1,0:T(8,128)(2,1)} %pad_maximum_fusion.6), channel_id=1, source_target_pairs={{0,2},{2,0},{4,6},{6,4},{8,10},{10,8},{12,14},{14,12},{16,18},{18,... | collective-permute-start | bytes 5308424 | tf_op jit(solution)/shard_map/ppermute | solution.py:263
  300.4 46.0 %collective-permute-start.20 = (bf16[3,2,2,2,48,256]{5,4,0,2,1,3:T(8,128)(2,1)}, bf16[3,2,2,2,48,256]{5,4,0,2,1,3:T(8,128)(2,1)}, u32[]{:S(2)}, u32[]{:S(2)}) collective-permute-start(bf16[3,2,2,2,48,256]{5,4,0,2,1,3:T(8,128)(2,1)} %fusion.59), channel_id=1, source_target_pairs={{0,2},{2,0},{4,6},{6,4},{8,10},{10,8},{12,14},{14,12},{16,18},{18,... | collective-permute-start | bytes 1769480 | tf_op jit(solution)/shard_map/ppermute | solution.py:263
  318.7 26.0 %collective-permute-start.25 = (bf16[2,2,2,48,768]{4,3,1,0,2:T(8,128)(2,1)}, bf16[2,2,2,48,768]{4,3,1,0,2:T(8,128)(2,1)}, u32[]{:S(2)}, u32[]{:S(2)}) collective-permute-start(bf16[2,2,2,48,768]{4,3,1,0,2:T(8,128)(2,1)} %fusion.61), channel_id=1, source_target_pairs={{0,2},{2,0},{4,6},{6,4},{8,10},{10,8},{12,14},{14,12},{16,18},{18,... | collective-permute-start | bytes 1769480 | tf_op jit(solution)/shard_map/ppermute | solution.py:263
  320.1 29.7 %collective-permute-start.15 = (bf16[3,2,2,2,48,256]{5,4,0,2,1,3:T(8,128)(2,1)}, bf16[3,2,2,2,48,256]{5,4,0,2,1,3:T(8,128)(2,1)}, u32[]{:S(2)}, u32[]{:S(2)}) collective-permute-start(bf16[3,2,2,2,48,256]{5,4,0,2,1,3:T(8,128)(2,1)} %fusion.58), channel_id=1, source_target_pairs={{0,2},{2,0},{4,6},{6,4},{8,10},{10,8},{12,14},{14,12},{16,18},{18,... | collective-permute-start | bytes 1769480 | tf_op jit(solution)/shard_map/ppermute | solution.py:263
  326.5 24.9 %collective-permute-start.10 = (bf16[3,2,2,2,48,256]{5,4,3,2,1,0:T(8,128)(2,1)S(1)}, bf16[3,2,2,2,48,256]{5,4,3,2,1,0:T(8,128)(2,1)S(1)}, u32[]{:S(2)}, u32[]{:S(2)}) collective-permute-start(bf16[3,2,2,2,48,256]{5,4,3,2,1,0:T(8,128)(2,1)S(1)} %fusion.57), channel_id=1, source_target_pairs={{0,2},{2,0},{4,6},{6,4},{8,10},{10,8},{12,14},{14,12},{16,18},{18,... | collective-permute-start | bytes 1769480 | tf_op jit(solution)/shard_map/ppermute | solution.py:263
  330.9 11.8 %collective-permute-start.44 = (f32[1,256]{1,0:T(1,128)S(1)}, f32[1,256]{1,0:T(1,128)S(1)}, u32[]{:S(2)}, u32[]{:S(2)}) collective-permute-start(f32[1,256]{1,0:T(1,128)S(1)} %fusion.123), channel_id=1, source_target_pairs={{0,8},{2,10},{4,12},{6,14},{8,0},{10,2},{12,4},{14,6},{16,24},{18,... | collective-permute-start | bytes 3080 | tf_op jit(solution)/shard_map/ppermute | solution.py:263
  342.7 47.0 %collective-permute-start.35 = (bf16[2,2,2,48,3072]{4,3,1,0,2:T(8,128)(2,1)}, bf16[2,2,2,48,3072]{4,3,1,0,2:T(8,128)(2,1)}, u32[]{:S(2)}, u32[]{:S(2)}) collective-permute-start(bf16[2,2,2,48,3072]{4,3,1,0,2:T(8,128)(2,1)} %fusion.11), channel_id=1, source_target_pairs={{0,2},{2,0},{4,6},{6,4},{8,10},{10,8},{12,14},{14,12},{16,18},{18,... | collective-permute-start | bytes 7077896 | tf_op jit(solution)/shard_map/ppermute | solution.py:263
  344.7 49.9 %collective-permute-start.30 = (bf16[2,2,2,48,3072]{4,3,1,0,2:T(8,128)(2,1)}, bf16[2,2,2,48,3072]{4,3,1,0,2:T(8,128)(2,1)S(1)}, u32[]{:S(2)}, u32[]{:S(2)}) collective-permute-start(bf16[2,2,2,48,3072]{4,3,1,0,2:T(8,128)(2,1)} %fusion.10), channel_id=1, source_target_pairs={{0,2},{2,0},{4,6},{6,4},{8,10},{10,8},{12,14},{14,12},{16,18},{18,... | collective-permute-start | bytes 7077896 | tf_op jit(solution)/shard_map/ppermute | solution.py:263
  346.5 9.9 %collective-permute-start.26 = (bf16[2,2,48,768]{3,2,1,0:T(8,128)(2,1)S(1)}, bf16[2,2,48,768]{3,2,1,0:T(8,128)(2,1)S(1)}, u32[]{:S(2)}, u32[]{:S(2)}) collective-permute-start(bf16[2,2,48,768]{3,2,1,0:T(8,128)(2,1)S(1)} %fusion.71), channel_id=1, source_target_pairs={{0,4},{2,6},{4,0},{6,2},{8,12},{10,14},{12,8},{14,10},{16,20},{18,... | collective-permute-start | bytes 884744 | tf_op jit(solution)/shard_map/ppermute | solution.py:263
  349.9 9.4 %collective-permute-start.21 = (bf16[3,2,2,2,48,128]{5,4,0,2,1,3:T(8,128)(2,1)S(1)}, bf16[3,2,2,2,48,128]{5,4,0,2,1,3:T(8,128)(2,1)S(1)}, u32[]{:S(2)}, u32[]{:S(2)}) collective-permute-start(bf16[3,2,2,2,48,128]{5,4,0,2,1,3:T(8,128)(2,1)S(1)} %dynamic-slice_convert_fusion.10), channel_id=1, source_target_pairs={{0,1},{1,0},{2,3},{3,2},{4,5},{5,4},{6,7},{7,6},{8,9},{9,8},{10,11... | collective-permute-start | bytes 884744 | tf_op jit(solution)/shard_map/ppermute | solution.py:261
  351.4 10.8 %collective-permute-start.16 = (bf16[3,2,2,48,256]{4,3,0,2,1:T(8,128)(2,1)S(1)}, bf16[3,2,2,48,256]{4,3,0,2,1:T(8,128)(2,1)S(1)}, u32[]{:S(2)}, u32[]{:S(2)}) collective-permute-start(bf16[3,2,2,48,256]{4,3,0,2,1:T(8,128)(2,1)S(1)} %fusion.70), channel_id=1, source_target_pairs={{0,4},{2,6},{4,0},{6,2},{8,12},{10,14},{12,8},{14,10},{16,20},{18,... | collective-permute-start | bytes 884744 | tf_op jit(solution)/shard_map/ppermute | solution.py:263
  356.4 9.9 %collective-permute-start.11 = (bf16[3,2,2,2,48,128]{5,4,3,2,1,0:T(8,128)(2,1)S(1)}, bf16[3,2,2,2,48,128]{5,4,3,2,1,0:T(8,128)(2,1)S(1)}, u32[]{:S(2)}, u32[]{:S(2)}) collective-permute-start(bf16[3,2,2,2,48,128]{5,4,3,2,1,0:T(8,128)(2,1)S(1)} %dynamic-slice_convert_fusion.12), channel_id=1, source_target_pairs={{0,1},{1,0},{2,3},{3,2},{4,5},{5,4},{6,7},{7,6},{8,9},{9,8},{10,11... | collective-permute-start | bytes 884744 | tf_op jit(solution)/shard_map/ppermute | solution.py:261
  359.2 10.2 %collective-permute-start.27 = (bf16[2,2,48,384]{3,2,1,0:T(8,128)(2,1)S(1)}, bf16[2,2,48,384]{3,2,1,0:T(8,128)(2,1)S(1)}, u32[]{:S(2)}, u32[]{:S(2)}) collective-permute-start(bf16[2,2,48,384]{3,2,1,0:T(8,128)(2,1)S(1)} %dynamic-slice_convert_fusion.15), channel_id=1, source_target_pairs={{0,1},{1,0},{2,3},{3,2},{4,5},{5,4},{6,7},{7,6},{8,9},{9,8},{10,11... | collective-permute-start | bytes 442376 | tf_op jit(solution)/shard_map/ppermute | solution.py:261
  370.6 9.4 %collective-permute-start.28 = (bf16[2,48,384]{2,1,0:T(8,128)(2,1)S(1)}, bf16[2,48,384]{2,1,0:T(8,128)(2,1)S(1)}, u32[]{:S(2)}, u32[]{:S(2)}) collective-permute-start(bf16[2,48,384]{2,1,0:T(8,128)(2,1)S(1)} %fusion.88), channel_id=1, source_target_pairs={{0,16},{2,18},{4,20},{6,22},{8,24},{10,26},{12,28},{14,30},{16,0},... | collective-permute-start | bytes 221192 | tf_op jit(solution)/shard_map/ppermute | solution.py:263
  374.6 8.6 %collective-permute-start.18 = (bf16[3,2,48,128]{3,2,0,1:T(8,128)(2,1)S(1)}, bf16[3,2,48,128]{3,2,0,1:T(8,128)(2,1)S(1)}, u32[]{:S(2)}, u32[]{:S(2)}) collective-permute-start(bf16[3,2,48,128]{3,2,0,1:T(8,128)(2,1)S(1)} %fusion.86), channel_id=1, source_target_pairs={{0,16},{2,18},{4,20},{6,22},{8,24},{10,26},{12,28},{14,30},{16,0},... | collective-permute-start | bytes 221192 | tf_op jit(solution)/shard_map/ppermute | solution.py:263
  381.7 15.2 %collective-permute-start.29 = (bf16[48,384]{1,0:T(8,128)(2,1)S(1)}, bf16[48,384]{1,0:T(8,128)(2,1)S(1)}, u32[]{:S(2)}, u32[]{:S(2)}) collective-permute-start(bf16[48,384]{1,0:T(8,128)(2,1)S(1)} %fusion.93), channel_id=1, source_target_pairs={{0,8},{2,10},{4,12},{6,14},{8,0},{10,2},{12,4},{14,6},{16,24},{18,... | collective-permute-start | bytes 110600 | tf_op jit(solution)/shard_map/ppermute | solution.py:263
  387.2 8.9 %collective-permute-start.14 = (bf16[3,48,128]{2,1,0:T(8,128)(2,1)S(1)}, bf16[3,48,128]{2,1,0:T(8,128)(2,1)S(1)}, u32[]{:S(2)}, u32[]{:S(2)}) collective-permute-start(bf16[3,48,128]{2,1,0:T(8,128)(2,1)S(1)} %fusion.90), channel_id=1, source_target_pairs={{0,8},{2,10},{4,12},{6,14},{8,0},{10,2},{12,4},{14,6},{16,24},{18,... | collective-permute-start | bytes 110600 | tf_op jit(solution)/shard_map/ppermute | solution.py:263
  393.6 24.2 %collective-permute-start.36 = (bf16[2,2,2,48,1536]{4,3,1,0,2:T(8,128)(2,1)S(1)}, bf16[2,2,2,48,1536]{4,3,1,0,2:T(8,128)(2,1)S(1)}, u32[]{:S(2)}, u32[]{:S(2)}) collective-permute-start(bf16[2,2,2,48,1536]{4,3,1,0,2:T(8,128)(2,1)S(1)} %dynamic-slice_convert_fusion), channel_id=1, source_target_pairs={{0,1},{1,0},{2,3},{3,2},{4,5},{5,4},{6,7},{7,6},{8,9},{9,8},{10,11... | collective-permute-start | bytes 3538952 | tf_op jit(solution)/shard_map/ppermute | solution.py:261
  395.8 26.0 %collective-permute-start.31 = (bf16[2,2,48,3072]{3,2,1,0:T(8,128)(2,1)S(1)}, bf16[2,2,48,3072]{3,2,1,0:T(8,128)(2,1)S(1)}, u32[]{:S(2)}, u32[]{:S(2)}) collective-permute-start(bf16[2,2,48,3072]{3,2,1,0:T(8,128)(2,1)S(1)} %fusion.41), channel_id=1, source_target_pairs={{0,4},{2,6},{4,0},{6,2},{8,12},{10,14},{12,8},{14,10},{16,20},{18,... | collective-permute-start | bytes 3538952 | tf_op jit(solution)/shard_map/ppermute | solution.py:263
  418.2 13.4 %collective-permute-start.37 = (bf16[2,2,48,1536]{3,2,1,0:T(8,128)(2,1)S(1)}, bf16[2,2,48,1536]{3,2,1,0:T(8,128)(2,1)S(1)}, u32[]{:S(2)}, u32[]{:S(2)}) collective-permute-start(bf16[2,2,48,1536]{3,2,1,0:T(8,128)(2,1)S(1)} %fusion.60), channel_id=1, source_target_pairs={{0,4},{2,6},{4,0},{6,2},{8,12},{10,14},{12,8},{14,10},{16,20},{18,... | collective-permute-start | bytes 1769480 | tf_op jit(solution)/shard_map/ppermute | solution.py:263
  422.2 11.1 %collective-permute-start.32 = (bf16[2,2,48,1536]{3,2,1,0:T(8,128)(2,1)S(1)}, bf16[2,2,48,1536]{3,2,1,0:T(8,128)(2,1)S(1)}, u32[]{:S(2)}, u32[]{:S(2)}) collective-permute-start(bf16[2,2,48,1536]{3,2,1,0:T(8,128)(2,1)S(1)} %dynamic-slice_convert_fusion.3), channel_id=1, source_target_pairs={{0,1},{1,0},{2,3},{3,2},{4,5},{5,4},{6,7},{7,6},{8,9},{9,8},{10,11... | collective-permute-start | bytes 1769480 | tf_op jit(solution)/shard_map/ppermute | solution.py:261
  431.8 20.2 %collective-permute-start.38 = (bf16[2,48,1536]{2,1,0:T(8,128)(2,1)S(1)}, bf16[2,48,1536]{2,1,0:T(8,128)(2,1)S(1)}, u32[]{:S(2)}, u32[]{:S(2)}) collective-permute-start(bf16[2,48,1536]{2,1,0:T(8,128)(2,1)S(1)} %fusion.73), channel_id=1, source_target_pairs={{0,16},{2,18},{4,20},{6,22},{8,24},{10,26},{12,28},{14,30},{16,0},... | collective-permute-start | bytes 884744 | tf_op jit(solution)/shard_map/ppermute | solution.py:263
  433.4 24.5 %collective-permute-start.33 = (bf16[2,48,1536]{2,1,0:T(8,128)(2,1)S(1)}, bf16[2,48,1536]{2,1,0:T(8,128)(2,1)S(1)}, u32[]{:S(2)}, u32[]{:S(2)}) collective-permute-start(bf16[2,48,1536]{2,1,0:T(8,128)(2,1)S(1)} %fusion.72), channel_id=1, source_target_pairs={{0,16},{2,18},{4,20},{6,22},{8,24},{10,26},{12,28},{14,30},{16,0},... | collective-permute-start | bytes 884744 | tf_op jit(solution)/shard_map/ppermute | solution.py:263
  452.1 9.0 %collective-permute-start.39 = (bf16[48,1536]{1,0:T(8,128)(2,1)S(1)}, bf16[48,1536]{1,0:T(8,128)(2,1)S(1)}, u32[]{:S(2)}, u32[]{:S(2)}) collective-permute-start(bf16[48,1536]{1,0:T(8,128)(2,1)S(1)} %fusion.84), channel_id=1, source_target_pairs={{0,8},{2,10},{4,12},{6,14},{8,0},{10,2},{12,4},{14,6},{16,24},{18,... | collective-permute-start | bytes 442376 | tf_op jit(solution)/shard_map/ppermute | solution.py:263
  (82 other events, 425.5 us)
Sparse Core Ops, SparseCore 0:
  11.2 97.2 all-gather.1
